TPU v7x, 256 devices: a whole 4x4x8 slice. The times are simulated.
256 devices in a mesh: node: 64 (over z, x, core), edge: 4 (over y).
Axes of the slice: x: 4, y: 4, z: 8, core: 2. Of those that a mesh axis runs over, the one named last changes fastest.
Arguments:
- teleport: float32 [131072, 128], P(('node', 'edge')), may hold values from -6 to 6
- cotangent: float32 [131072, 128], P(('node', 'edge')), may hold values from -6 to 6
- fetch_table: int32 [64, 128], replicated, may hold values from -1 to 7, as said below
- block_row: int32 [64, 192], P('node'), may hold values from 0 to 7
- block_slot: int32 [64, 192], P('node'), may hold values from 0 to 127, as said below
- values: bfloat16 [64, 192, 256, 256], P('node', None, 'edge'), may hold values from -0.078125 to 0.078125
Outputs:
- propagated: float32 [131072, 128], P(('node', 'edge'))
- teleport_grad: float32 [131072, 128], P(('node', 'edge'))
Inputs may be any that keep to these rules, and one draw needn't show every extreme that they name: `fetch_table`: entry n, o * 2 + k names a node block index j of owner group o that group n reads in slot k, or is -1 for an empty slot. Within the 2 slots of one owner the live ones come first and name distinct blocks. One owner group has all 2 slots live in every row. `block_slot`: every entry names a live slot of the group's row of fetch_table, and every live slot of that row is named by at least one adjacency block of the group.
All inputs are finite; a program needn't handle non-finite values.
Results may differ from a plain program's by a relative error of at most 0.004.
Values may be sent and summed in bfloat16 or wider, within the bound.
A program may use at most 128 MiB of HBM per device.

v0:
```python
import jax
import jax.numpy as jnp
from jax import lax
from jax.sharding import PartitionSpec as P

CAP = 2
STEPS = 2


def per_device(teleport, cotangent, fetch_table, block_row, block_slot, values):
    row_count, hidden = teleport.shape
    quarter = values.shape[2]
    block_count = values.shape[1]
    blocks_dev = row_count // quarter
    slot_total = fetch_table.shape[1]
    owner_count = lax.axis_size("node")
    group_size = 16
    turn_count = block_count // group_size
    owner_index = lax.axis_index("node")
    local_weights = values[0]
    row_ids = block_row[0]
    slot_ids = block_slot[0]
    own_plan = lax.dynamic_index_in_dim(fetch_table, owner_index, 0, keepdims=False)
    local_ids = jnp.take(own_plan, slot_ids, axis=0)
    global_ids = slot_ids // CAP * blocks_dev + local_ids
    requests = lax.dynamic_slice_in_dim(fetch_table, owner_index * CAP, CAP, 1).reshape(slot_total)
    block_range = jnp.arange(blocks_dev, dtype=jnp.int32)
    request_hot = requests[:, None] == block_range[None, :]
    request_float = request_hot.astype(jnp.float32)
    weight_groups = local_weights.reshape(turn_count, group_size, quarter, local_weights.shape[2])
    row_groups = row_ids.reshape(turn_count, group_size)
    slot_groups = slot_ids.reshape(turn_count, group_size)
    current = teleport
    for step_index in range(STEPS):
        propagate_rounded = current.astype(jnp.bfloat16)
        everything = lax.all_gather(propagate_rounded, "node", axis=0, tiled=True)
        feature_table = everything.reshape(owner_count * blocks_dev, quarter, hidden)
        columns = jnp.take(feature_table, global_ids, axis=0)
        column_groups = columns.reshape(turn_count, group_size, quarter, hidden)

        def partial_rows(amount):
            quarters_used = amount // row_count

            def partial_advance(running, inputs):
                weights, sources, targets = inputs
                product = jnp.einsum(
                    "bcr,bch->brh", weights, sources, preferred_element_type=jnp.float32
                )
                product = product.reshape(group_size, quarters_used, quarter, hidden)
                return (running.at[targets].add(product), None)

            start_sum = jnp.zeros((blocks_dev, quarters_used, quarter, hidden), jnp.float32)
            running, _ = lax.scan(
                partial_advance, start_sum, (weight_groups, column_groups, row_groups)
            )
            return running.transpose(1, 0, 2, 3).reshape(amount, hidden)

        current = (
            0.9
            * lax.psum_scatter(
                partial_rows(lax.axis_size("edge") * row_count),
                "edge",
                scatter_dimension=0,
                tiled=True,
            )
            + 0.1 * teleport
        )
    adjoint = cotangent
    gradient = 0.1 * cotangent
    for step_index in range(STEPS):
        rounded = adjoint.astype(jnp.bfloat16).reshape(blocks_dev, quarter, hidden)

        def fold_rows(running, arrived_rows):

            def fold_advance(carried, inputs):
                weights, targets, slot_targets = inputs
                sources = jnp.take(arrived_rows, targets, axis=0)
                product = jnp.einsum(
                    "bcr,brh->bch", weights, sources, preferred_element_type=jnp.float32
                )
                return (carried.at[slot_targets].add(product), None)

            carried, _ = lax.scan(fold_advance, running, (weight_groups, row_groups, slot_groups))
            return carried

        transpose_start_sum = jnp.zeros((slot_total, quarter, hidden), jnp.float32)
        partial_value = fold_rows(
            transpose_start_sum, lax.all_gather(rounded, "edge", axis=1, tiled=True)
        )
        summed = jnp.einsum(
            "sj,sch->jch",
            request_float,
            lax.all_to_all(partial_value, "node", split_axis=0, concat_axis=0, tiled=True),
            precision=lax.Precision.HIGHEST,
        )
        adjoint = 0.9 * summed.reshape(row_count, hidden)
        factor = 0.1 if step_index + 1 < STEPS else 1.0
        gradient = gradient + factor * adjoint
    return (current, gradient)


def solution(mesh):
    placed = (
        P(("node", "edge"), None),
        P(("node", "edge"), None),
        P(),
        P("node", None),
        P("node", None),
        P("node", None, "edge", None),
    )
    return jax.shard_map(
        per_device,
        mesh=mesh,
        in_specs=placed,
        out_specs=(P(("node", "edge"), None), P(("node", "edge"), None)),
        check_vma=False,
    )
```

profile of v0, /device:TPU:1, one launch (start us, length us, event | category | flops | bytes accessed | tf_op | source)
XLA Modules:
  0.0 394.2 jit_solution(16684911462658416126)
XLA Ops:
  13.2 12.6 %all_gather.14 = bf16[8,256,128]{2,1,0:T(8,128)(2,1)S(1)} all-gather(bf16[8,64,128]{2,1,0:T(8,128)(2,1)S(1)} %bitcast.133), channel_id=1, replica_groups=mesh['node'=64,'edge'=4] {'edge'}, dimensions={1}, use_global_device_ids=true | all-gather | bytes 655360 | tf_op jit(solution)/shard_map/all_gather | solution.py:88
  25.8 2.5 broadcast.151.clone
  28.3 59.0 %while.42 = (s32[]{:T(128)}, f32[128,64,128]{2,1,0:T(8,128)}, s32[12,16]{1,0:T(8,128)S(1)}, bf16[12,16,64,256]{3,2,1,0:T(8,128)(2,1)}, s32[12,16]{1,0:T(8,128)S(1)}, /*index=5*/bf16[8,256,128]{2,1,0:T(8,128)(2,1)S(1)}, s32[]{:T(128)}) while((s32[]{:T(128)}, f32[128,64,128]{2,1,0:T(8,128)}, s32[12,16]{1,0:T(8,128)S(1)}, ...), condition=%wide.region_10.13_spmd, body=%wide.region_8.12_spmd.sunk | while | flops 67765392 | bytes 5772341 | solution.py:83
  30.5 2.7 scatter_fusion.2
  35.4 2.7 scatter_fusion.2
  40.4 2.7 scatter_fusion.2
  45.3 2.7 scatter_fusion.2
  50.2 2.7 scatter_fusion.2
  55.1 2.7 scatter_fusion.2
  60.0 2.7 scatter_fusion.2
  64.9 2.7 scatter_fusion.2
  69.8 2.7 scatter_fusion.2
  74.7 2.7 scatter_fusion.2
  79.7 2.7 scatter_fusion.2
  84.6 2.7 scatter_fusion.2
  87.3 14.1 %all-to-all-start = ((f32[128,64,128]{2,1,0:T(8,128)}), f32[128,64,128]{2,1,0:T(8,128)}, u32[]{:S(2)}, u32[]{:S(2)}) async-start(f32[128,64,128]{2,1,0:T(8,128)} %get-tuple-element.124), calls=%async_computation.2 | async-start | bytes 8388608 | tf_op jit(solution)/shard_map/all_to_all | solution.py:93
  103.2 4.5 %gather_fusion.3 = bf16[192,64,128]{2,1,0:T(8,128)(2,1)S(1)} fusion(bf16[512,64,128]{2,1,0:T(8,128)(2,1)} %bitcast.131, s32[1024]{0:T(1024)S(1)} %pad_clamp_fusion.2), kind=kCustom, calls=%fused_computation.clone | custom fusion | bytes 6292224 | tf_op jit(solution)/shard_map/jit(_take)/gather | solution.py:38
  109.9 46.1 %while.40 = (s32[]{:T(128)}, f32[8,4,64,128]{3,2,1,0:T(8,128)S(1)}, s32[12,16]{1,0:T(8,128)S(1)}, bf16[12,16,64,256]{3,2,1,0:T(8,128)(2,1)}, bf16[12,16,64,128]{3,2,1,0:T(8,128)(2,1)}, /*index=5*/s32[]{:T(128)}) while((s32[]{:T(128)}, f32[8,4,64,128]{3,2,1,0:T(8,128)S(1)}, s32[12,16]{1,0:T(8,128)S(1)}, bf16[12,16,64,256]{3,2,1,0:T(8,128)(2,1)}, ...), condition=%wide.region_2.4_spmd, body=%wide.region_0.0_spmd.sunk | while | flops 67633200 | bytes 9176329 | solution.py:53
  111.6 2.2 scatter_fusion
  115.4 2.2 scatter_fusion
  119.3 2.2 scatter_fusion
  123.1 2.2 scatter_fusion
  126.9 2.2 scatter_fusion
  130.8 2.2 scatter_fusion
  134.6 2.2 scatter_fusion
  138.4 2.2 scatter_fusion
  142.3 2.2 scatter_fusion
  146.1 2.2 scatter_fusion
  150.0 2.2 scatter_fusion
  153.8 2.2 scatter_fusion
  157.1 25.6 %reduce-scatter.3.cloned.1.call-done = f32[512,128]{1,0:T(8,128)} async-done(((f32[2048,128]{1,0:T(8,128)}), f32[512,128]{1,0:T(8,128)}) %reduce-scatter.3.cloned.1.call-update) | async-done | bytes 262160 | tf_op jit(solution)/shard_map/reduce_scatter | solution.py:60
  184.7 11.2 %all-to-all-done = f32[128,64,128]{2,1,0:T(8,128)} async-done(((f32[128,64,128]{2,1,0:T(8,128)}), f32[128,64,128]{2,1,0:T(8,128)}, u32[]{:S(2)}, u32[]{:S(2)}) %all-to-all-start) | async-done | bytes 4194336 | tf_op jit(solution)/shard_map/all_to_all | solution.py:93
  195.9 6.5 %broadcast_multiply_fusion = (f32[8,64,128]{2,0,1:T(8,128)}, bf16[8,64,128]{2,0,1:T(8,128)(2,1)S(1)}) fusion(f32[128,64,128]{2,1,0:T(8,128)} %all-to-all-done, s32[128]{0:T(128)S(1)} %eq.15), kind=kOutput, calls=%fused_computation.75 | convolution fusion | flops 100860928 | bytes 4588032 | tf_op jit(solution)/shard_map/sj,sch->jch/dot_general | solution.py:90
  202.3 10.6 %all_gather.15 = bf16[8,256,128]{2,0,1:T(8,128)(2,1)S(1)} all-gather(bf16[8,64,128]{2,0,1:T(8,128)(2,1)S(1)} %get-tuple-element.195), channel_id=1, replica_groups=mesh['node'=64,'edge'=4] {'edge'}, dimensions={1}, use_global_device_ids=true | all-gather | bytes 655360 | tf_op jit(solution)/shard_map/all_gather | solution.py:88
  213.0 2.5 broadcast.151
  215.5 59.0 %while.43 = (s32[]{:T(128)}, f32[128,64,128]{2,1,0:T(8,128)}, s32[12,16]{1,0:T(8,128)S(1)}, bf16[12,16,64,256]{3,2,1,0:T(8,128)(2,1)}, s32[12,16]{1,0:T(8,128)S(1)}, /*index=5*/bf16[8,256,128]{2,1,0:T(8,128)(2,1)S(1)}, s32[]{:T(128)}) while((s32[]{:T(128)}, f32[128,64,128]{2,1,0:T(8,128)}, s32[12,16]{1,0:T(8,128)S(1)}, ...), condition=%wide.region_13.16_spmd, body=%wide.region_11.15_spmd.sunk | while | flops 67765392 | bytes 5772341 | solution.py:83
  217.7 2.7 scatter_fusion.3
  222.6 2.7 scatter_fusion.3
  227.5 2.7 scatter_fusion.3
  232.4 2.7 scatter_fusion.3
  237.3 2.7 scatter_fusion.3
  242.2 2.7 scatter_fusion.3
  247.2 2.7 scatter_fusion.3
  252.1 2.8 scatter_fusion.3
  257.1 2.7 scatter_fusion.3
  262.0 2.7 scatter_fusion.3
  266.9 2.7 scatter_fusion.3
  271.8 2.7 scatter_fusion.3
  274.5 10.5 %all-to-all-start.1 = ((f32[128,64,128]{2,1,0:T(8,128)}), f32[128,64,128]{2,1,0:T(8,128)}, u32[]{:S(2)}, u32[]{:S(2)}) async-start(f32[128,64,128]{2,1,0:T(8,128)} %get-tuple-element.125), calls=%async_computation.3 | async-start | bytes 8388608 | tf_op jit(solution)/shard_map/all_to_all | solution.py:93
  285.0 4.5 %gather_fusion.4 = bf16[192,64,128]{2,1,0:T(8,128)(2,1)S(1)} fusion(bf16[512,64,128]{2,1,0:T(8,128)(2,1)} %bitcast.132, s32[1024]{0:T(1024)S(1)} %pad_clamp_fusion.2), kind=kCustom, calls=%fused_computation.2.clone | custom fusion | bytes 6292224 | tf_op jit(solution)/shard_map/jit(_take)/gather | solution.py:38
  291.8 46.0 %while.41 = (s32[]{:T(128)}, f32[8,4,64,128]{3,2,1,0:T(8,128)S(1)}, s32[12,16]{1,0:T(8,128)S(1)}, bf16[12,16,64,256]{3,2,1,0:T(8,128)(2,1)}, bf16[12,16,64,128]{3,2,1,0:T(8,128)(2,1)}, /*index=5*/s32[]{:T(128)}) while((s32[]{:T(128)}, f32[8,4,64,128]{3,2,1,0:T(8,128)S(1)}, s32[12,16]{1,0:T(8,128)S(1)}, bf16[12,16,64,256]{3,2,1,0:T(8,128)(2,1)}, ...), condition=%wide.region_6.8_spmd, body=%wide.region_4.7_spmd.sunk | while | flops 67633200 | bytes 9176329 | solution.py:53
  293.4 2.2 scatter_fusion.1
  301.1 2.2 scatter_fusion.1
  304.9 2.2 scatter_fusion.1
  308.7 2.2 scatter_fusion.1
  312.6 2.2 scatter_fusion.1
  316.4 2.2 scatter_fusion.1
  320.3 2.2 scatter_fusion.1
  324.1 2.2 scatter_fusion.1
  327.9 2.2 scatter_fusion.1
  331.8 2.2 scatter_fusion.1
  335.6 2.2 scatter_fusion.1
  339.9 39.5 %all-to-all-done.1 = f32[128,64,128]{2,1,0:T(8,128)} async-done(((f32[128,64,128]{2,1,0:T(8,128)}), f32[128,64,128]{2,1,0:T(8,128)}, u32[]{:S(2)}, u32[]{:S(2)}) %all-to-all-start.1) | async-done | bytes 4194336 | tf_op jit(solution)/shard_map/all_to_all | solution.py:93
  379.4 5.8 %fusion.42 = f32[8,64,128]{2,0,1:T(8,128)S(1)} fusion(f32[128,64,128]{2,1,0:T(8,128)} %all-to-all-done.1, s32[128]{0:T(128)S(1)} %eq.15), kind=kOutput, calls=%fused_computation.69 | convolution fusion | flops 100729856 | bytes 4456960 | tf_op jit(solution)/shard_map/sj,sch->jch/dot_general | solution.py:90
  (217 shorter events, 113.4 us)
Async XLA Ops:
  7.2 94.3 %copy-start = (s32[64,128]{1,0:T(8,128)S(1)}, s32[64,128]{1,0:T(8,128)}, u32[]{:S(2)}) copy-start(s32[64,128]{1,0:T(8,128)} %param.20) | copy-start | bytes 98308
  7.2 96.0 %all-gather.3.cloned.1.call-start = ((), (), s32[]{:S(2)}) async-start(), calls=%async_computation.4 | async-start | bytes 8519680 | tf_op jit(solution)/shard_map/all_gather | solution.py:36
  87.3 14.2 %copy-start.4 = (s32[1,192]{1,0:T(1,128)S(1)}, s32[1,192]{1,0:T(1,128)}, u32[]{:S(2)}) copy-start(s32[1,192]{1,0:T(1,128)} %param.22) | copy-start | bytes 2308
  87.3 108.6 %all-to-all-start = ((f32[128,64,128]{2,1,0:T(8,128)}), f32[128,64,128]{2,1,0:T(8,128)}, u32[]{:S(2)}, u32[]{:S(2)}) async-start(f32[128,64,128]{2,1,0:T(8,128)} %get-tuple-element.124), calls=%async_computation.2 | async-start | bytes 8388608 | tf_op jit(solution)/shard_map/all_to_all | solution.py:93
  101.4 81.3 %reduce-scatter.3.cloned.1.call-start = ((), (), s32[]{:S(2)}) async-start(), calls=%async_computation.5 | async-start | bytes 1310720 | tf_op jit(solution)/shard_map/reduce_scatter | solution.py:60
  109.9 72.9 %copy-start.2 = (f32[512,128]{1,0:T(8,128)S(1)}, f32[512,128]{1,0:T(8,128)}, u32[]{:S(2)}) copy-start(f32[512,128]{1,0:T(8,128)} %param.18) | copy-start | bytes 786436
  157.1 128.0 %all-gather.5.cloned.1.call-start = ((), (), s32[]{:S(2)}) async-start(), calls=%async_computation.6 | async-start | bytes 8519680 | tf_op jit(solution)/shard_map/all_gather | solution.py:36
  274.5 104.9 %all-to-all-start.1 = ((f32[128,64,128]{2,1,0:T(8,128)}), f32[128,64,128]{2,1,0:T(8,128)}, u32[]{:S(2)}, u32[]{:S(2)}) async-start(f32[128,64,128]{2,1,0:T(8,128)} %get-tuple-element.125), calls=%async_computation.3 | async-start | bytes 8388608 | tf_op jit(solution)/shard_map/all_to_all | solution.py:93
  285.0 101.0 %reduce-scatter.5.cloned.1.call-start = ((), (), s32[]{:S(2)}) async-start(), calls=%async_computation.7 | async-start | bytes 1310720 | tf_op jit(solution)/shard_map/reduce_scatter | solution.py:60
  337.8 47.4 %copy-start.3 = (f32[512,128]{1,0:T(8,128)S(1)}, f32[512,128]{1,0:T(8,128)}, u32[]{:S(2)}) copy-start(f32[512,128]{1,0:T(8,128)} %param.19) | copy-start | bytes 786436
  338.9 48.8 %copy-start.1 = (s32[64,128]{1,0:T(8,128)S(1)}, s32[64,128]{1,0:T(8,128)}, u32[]{:S(2)}) copy-start(s32[64,128]{1,0:T(8,128)} %param.20) | copy-start | bytes 98308
Sparse Core Ops, SparseCore 0:
  11.4 87.1 all-gather.2
  157.2 25.5 reduce-scatter.2
  186.5 84.6 all-gather.4
  339.0 25.6 reduce-scatter.4
where the time goes:
time: 400 us; the launch traced here: 394 us
  other arithmetic  132 us (33%)
  matrix products  84.7 us (21%)
  waiting for transfers between devices  76.4 us (19%)
  local copies, waits for them, and re-layouts  38 us (10%)
  starting transfers between devices  24.8 us (6%)
  blocking collectives  23.2 us (6%)
  between operations  14 us (4%)
    scatter-add x24, other arithmetic, fold_advance(): return (carried.at[slot_targets].add(product), None)  64.4 us
    scatter-add x24, other arithmetic, partial_advance(): return (running.at[targets].add(product), None)  52.7 us
    all_to_all x2, waiting for transfers between devices, per_device(): lax.all_to_all(partial_value, 'node', split_axis=0, concat_axis=0, tiled=...  50.7 us
    dot_general x24, matrix products, partial_advance(): jnp.einsum('bcr,bch->brh', weights, sources, preferred_element_type=jnp.f...  38.3 us
    dot_general x24, matrix products, fold_advance(): jnp.einsum('bcr,brh->bch', weights, sources, preferred_element_type=jnp.f...  34.2 us
    reduce_scatter x2, waiting for transfers between devices, per_device(): lax.psum_scatter(partial_rows(lax.axis_size('edge') * row_count), 'edge',...  25.6 us
    all_to_all x2, starting transfers between devices, per_device(): lax.all_to_all(partial_value, 'node', split_axis=0, concat_axis=0, tiled=...  24.6 us
    all_gather x2, blocking collectives, per_device(): lax.all_gather(rounded, 'edge', axis=1, tiled=True)  23.2 us
  transfers between devices with their start and end apart: 6, of which 3 were waited for; matrix products, arithmetic and copies ran while one was open for 64% of the time, Pallas kernels for 0%

commit v1 on v0

v1 whole, which is shorter than its diff:
```python
import functools

import jax
import jax.numpy as jnp
from jax import lax
from jax.experimental import pallas as pl
from jax.experimental.pallas import tpu as pltpu
from jax.sharding import Mesh
from jax.sharding import PartitionSpec as P

CAP = 2
STEPS = 2
Z_SIZE = 8
X_SIZE = 4
CORE_SIZE = 2
CHUNK = 16


def forward_kernel(rows_ref, slots_ref, v_ref, x_ref, out_ref):
    step = pl.program_id(0)

    @pl.when(step == 0)
    def _():
        out_ref[...] = jnp.zeros_like(out_ref)

    quarters, _, quarter, hidden = out_ref.shape

    def body(i, carry):
        b = step * CHUNK + i
        j = rows_ref[b]
        s = slots_ref[b]
        product = lax.dot_general(
            v_ref[i], x_ref[s], (((0,), (0,)), ((), ())), preferred_element_type=jnp.float32
        )
        out_ref[:, j] += product.reshape(quarters, quarter, hidden)
        return carry

    lax.fori_loop(0, CHUNK, body, 0)


def backward_kernel(rows_ref, slots_ref, v_ref, a_ref, out_ref):
    step = pl.program_id(0)

    @pl.when(step == 0)
    def _():
        out_ref[...] = jnp.zeros_like(out_ref)

    quarters, _, quarter, hidden = a_ref.shape

    def body(i, carry):
        b = step * CHUNK + i
        j = rows_ref[b]
        s = slots_ref[b]
        sources = a_ref[:, j].reshape(quarters * quarter, hidden)
        out_ref[s] += jnp.dot(v_ref[i], sources, preferred_element_type=jnp.float32)
        return carry

    lax.fori_loop(0, CHUNK, body, 0)


def forward_apply(rows, slots, weights, received, quarters):
    block_count, quarter, width = weights.shape
    hidden = received.shape[-1]
    blocks_dev = 8
    return pl.pallas_call(
        forward_kernel,
        out_shape=jax.ShapeDtypeStruct((quarters, blocks_dev, quarter, hidden), jnp.float32),
        grid_spec=pltpu.PrefetchScalarGridSpec(
            num_scalar_prefetch=2,
            grid=(block_count // CHUNK,),
            in_specs=[
                pl.BlockSpec((CHUNK, quarter, width), lambda i, r, s: (i, 0, 0)),
                pl.BlockSpec(received.shape, lambda i, r, s: (0, 0, 0)),
            ],
            out_specs=pl.BlockSpec(
                (quarters, blocks_dev, quarter, hidden), lambda i, r, s: (0, 0, 0, 0)
            ),
        ),
        compiler_params=pltpu.CompilerParams(dimension_semantics=("arbitrary",)),
    )(rows, slots, weights, received)


def backward_apply(rows, slots, weights, sources, slot_total):
    block_count, quarter, width = weights.shape
    hidden = sources.shape[-1]
    return pl.pallas_call(
        backward_kernel,
        out_shape=jax.ShapeDtypeStruct((slot_total, quarter, hidden), jnp.float32),
        grid_spec=pltpu.PrefetchScalarGridSpec(
            num_scalar_prefetch=2,
            grid=(block_count // CHUNK,),
            in_specs=[
                pl.BlockSpec((CHUNK, quarter, width), lambda i, r, s: (i, 0, 0)),
                pl.BlockSpec(sources.shape, lambda i, r, s: (0, 0, 0, 0)),
            ],
            out_specs=pl.BlockSpec((slot_total, quarter, hidden), lambda i, r, s: (0, 0, 0)),
        ),
        compiler_params=pltpu.CompilerParams(dimension_semantics=("arbitrary",)),
    )(rows, slots, weights, sources)


def per_device(teleport, cotangent, fetch_table, block_row, block_slot, values):
    row_count, hidden = teleport.shape
    quarter = values.shape[2]
    blocks_dev = row_count // quarter
    slot_total = fetch_table.shape[1]
    quarters = lax.axis_size("edge")
    row_peers = X_SIZE * CORE_SIZE
    z_me = lax.axis_index("z")
    x_me = lax.axis_index("x")
    c_me = lax.axis_index("c")
    weights = values[0]
    row_ids = block_row[0]
    slot_ids = block_slot[0]

    owner = slot_ids // CAP
    placed_slots = (
        ((owner // CORE_SIZE % X_SIZE * CORE_SIZE + owner % CORE_SIZE) * Z_SIZE + owner // (CORE_SIZE * X_SIZE))
        * CAP
        + slot_ids % CAP
    ).astype(jnp.int32)

    peer_range = jnp.arange(row_peers, dtype=jnp.int32)
    z_range = jnp.arange(Z_SIZE, dtype=jnp.int32)
    peer_groups = (z_me * X_SIZE + peer_range // CORE_SIZE) * CORE_SIZE + peer_range % CORE_SIZE
    line_owners = (z_range * X_SIZE + x_me) * CORE_SIZE + c_me
    table_cols = line_owners[:, None] * CAP + jnp.arange(CAP, dtype=jnp.int32)[None, :]
    wanted = fetch_table[peer_groups[:, None, None], table_cols[None, :, :]]
    send_index = (z_range[None, :, None] * blocks_dev + jnp.maximum(wanted, 0)).reshape(-1)
    wanted_hot = (
        wanted.transpose(1, 0, 2).reshape(Z_SIZE, 1, row_peers * CAP)
        == jnp.arange(blocks_dev, dtype=jnp.int32)[None, :, None]
    ).astype(jnp.float32)

    current = teleport
    for step_index in range(STEPS):
        rounded = current.astype(jnp.bfloat16).reshape(blocks_dev, quarter, hidden)
        line_blocks = lax.all_gather(rounded, "z", axis=0, tiled=True)
        outgoing = jnp.take(line_blocks, send_index, axis=0)
        received = lax.all_to_all(
            outgoing, ("x", "c"), split_axis=0, concat_axis=0, tiled=True
        )
        partial = forward_apply(row_ids, placed_slots, weights, received, quarters)
        summed = lax.psum_scatter(
            partial.reshape(quarters * row_count, hidden), "edge", scatter_dimension=0, tiled=True
        )
        current = 0.9 * summed + 0.1 * teleport

    adjoint = cotangent
    gradient = 0.1 * cotangent
    for step_index in range(STEPS):
        rounded = adjoint.astype(jnp.bfloat16).reshape(1, blocks_dev, quarter, hidden)
        whole_rows = lax.all_gather(rounded, "edge", axis=0, tiled=True)
        slot_sums = backward_apply(row_ids, placed_slots, weights, whole_rows, slot_total)
        arrived = lax.all_to_all(
            slot_sums, ("x", "c"), split_axis=0, concat_axis=0, tiled=True
        )
        arrived = arrived.reshape(row_peers, Z_SIZE, CAP, quarter * hidden)
        arrived = arrived.transpose(1, 0, 2, 3).reshape(Z_SIZE, row_peers * CAP, quarter * hidden)
        dense = jnp.einsum(
            "zjq,zqd->zjd", wanted_hot, arrived, precision=lax.Precision.HIGHEST
        )
        owned = lax.psum_scatter(dense, "z", scatter_dimension=0, tiled=True)
        adjoint = 0.9 * owned.reshape(row_count, hidden)
        factor = 0.1 if step_index + 1 < STEPS else 1.0
        gradient = gradient + factor * adjoint
    return (current, gradient)


def solution(mesh):
    devices = mesh.devices.reshape(Z_SIZE, X_SIZE, CORE_SIZE, mesh.shape["edge"])
    fine = Mesh(devices, ("z", "x", "c", "edge"))
    node = ("z", "x", "c")
    placed = (
        P((*node, "edge"), None),
        P((*node, "edge"), None),
        P(),
        P(node, None),
        P(node, None),
        P(node, None, "edge", None),
    )
    return jax.shard_map(
        per_device,
        mesh=fine,
        in_specs=placed,
        out_specs=(P((*node, "edge"), None), P((*node, "edge"), None)),
        check_vma=False,
    )
```

time: 400 us -> 464 us (1.16)
  Pallas kernels: 0 us -> 146 us
  other arithmetic: 132 us -> 11.8 us
  waiting for transfers between devices: 76.4 us -> 177 us
  matrix products: 84.7 us -> 10.1 us
  starting transfers between devices: 24.8 us -> 34.7 us
    pallas_call x0 -> x4, Pallas kernels: none -> 146 us  [the longest x2 83.3 us: forward_apply(): pl.pallas_call(forward_kernel, out_shape=jax.ShapeDtypeStruct((quarters,...]
    scatter-add x48 -> x0, other arithmetic: 117 us -> none  [the longest x24 64.4 us: fold_advance(): return (carried.at[slot_targets].add(product), None)]
    dot_general x50 -> x2, matrix products: 84.7 us -> 10.1 us  [per_device(): jnp.einsum('zjq,zqd->zjd', wanted_hot, arrived, precision=lax.Precision.H...]
    all_gather x2, waiting for transfers between devices: 0.04 us -> 37 us  [per_device(): line_blocks = lax.all_gather(rounded, 'z', axis=0, tiled=True)]
    reduce_scatter x2 -> x4, waiting for transfers between devices: 25.6 us -> 59.9 us  [the longest x2 59.9 us: per_device(): owned = lax.psum_scatter(dense, 'z', scatter_dimension=0, tiled=True)]
    all_to_all x2 -> x4, waiting for transfers between devices: 50.7 us -> 79.9 us  [the longest x2 54.2 us: per_device(): lax.all_to_all(slot_sums, ('x', 'c'), split_axis=0, concat_axis=0, tiled=...]
    reshape x0 -> x4, local copies, waits for them, and re-layouts: none -> 24 us  [the longest x2 12.2 us: per_device(): arrived.transpose(1, 0, 2, 3)]
    gather x27 -> x4, local copies, waits for them, and re-layouts: 28.6 us -> 5.72 us  [the longest x2 4.35 us: per_device(): outgoing = jnp.take(line_blocks, send_index, axis=0)]
  transfers between devices with their start and end apart: 6 -> 10, of which waited for: 3 -> 6; matrix products, arithmetic and copies ran while one was open for 64% -> 12% of each run, Pallas kernels for 0% -> 23%
where the time goes in v1:
time: 464 us; the launch traced here: 460 us
  waiting for transfers between devices  177 us (38%)
  Pallas kernels  146 us (31%)
  local copies, waits for them, and re-layouts  42.4 us (9%)
  starting transfers between devices  34.7 us (7%)
  blocking collectives  23.8 us (5%)
  between operations  14.3 us (3%)
  other arithmetic  11.8 us (3%)
  matrix products  10.1 us (2%)
    pallas_call x2, Pallas kernels, forward_apply(): pl.pallas_call(forward_kernel, out_shape=jax.ShapeDtypeStruct((quarters,...  83.3 us
    pallas_call x2, Pallas kernels, backward_apply(): pl.pallas_call(backward_kernel, out_shape=jax.ShapeDtypeStruct((slot_tota...  62.5 us
    reduce_scatter x2, waiting for transfers between devices, per_device(): owned = lax.psum_scatter(dense, 'z', scatter_dimension=0, tiled=True)  59.9 us
    all_to_all x2, waiting for transfers between devices, per_device(): lax.all_to_all(slot_sums, ('x', 'c'), split_axis=0, concat_axis=0, tiled=...  54.2 us
    all_gather x2, waiting for transfers between devices, per_device(): line_blocks = lax.all_gather(rounded, 'z', axis=0, tiled=True)  37 us
    all_to_all x2, waiting for transfers between devices, per_device(): lax.all_to_all(outgoing, ('x', 'c'), split_axis=0, concat_axis=0, tiled=T...  25.7 us
    all_gather x2, blocking collectives, per_device(): whole_rows = lax.all_gather(rounded, 'edge', axis=0, tiled=True)  23.8 us
    all_to_all x2, starting transfers between devices, per_device(): lax.all_to_all(slot_sums, ('x', 'c'), split_axis=0, concat_axis=0, tiled=...  20 us
  transfers between devices with their start and end apart: 10, of which 6 were waited for; matrix products, arithmetic and copies ran while one was open for 12% of the time, Pallas kernels for 23%

profile of v1, /device:TPU:1, one launch (start us, length us, event | category | flops | bytes accessed | tf_op | source)
XLA Modules:
  0.0 459.8 jit_solution(9413498404841068094)
XLA Ops:
  7.2 0.0 copy-start
  7.2 0.0 all-gather.3.cloned.1.call-start
  7.2 1.6 convert_element_type.23
  8.8 0.0 all-gather.3.cloned.1.call-update
  8.9 0.1 fusion.6
  9.0 0.1 broadcast_or_fusion
  9.1 0.1 reshape.131
  9.2 0.0 copy-done
  9.2 1.2 gather_fusion
  10.5 0.1 reshape.134
  10.6 0.1 maximum_add_fusion
  10.7 0.1 add.163
  10.9 37.0 %all-gather.3.cloned.1.call-done = bf16[64,64,128]{2,1,0:T(8,128)(2,1)} async-done(((bf16[8,64,128]{2,1,0:T(8,128)(2,1)}), bf16[64,64,128]{2,1,0:T(8,128)(2,1)}) %all-gather.3.cloned.1.call-update) | async-done | bytes 1048592 | tf_op jit(solution)/shard_map/all_gather | solution.py:138
  47.8 2.2 gather_fusion.1
  50.0 1.6 broadcast_select_fusion
  51.6 10.2 %all-to-all-start = ((bf16[128,64,128]{2,1,0:T(8,128)(2,1)}), bf16[128,64,128]{2,1,0:T(8,128)(2,1)S(1)}, u32[]{:S(2)}, u32[]{:S(2)}) async-start(bf16[128,64,128]{2,1,0:T(8,128)(2,1)} %broadcast_select_fusion), calls=%async_computation | async-start | bytes 4194304 | tf_op jit(solution)/shard_map/all_to_all | solution.py:140
  61.8 0.0 reduce-scatter.5.cloned.1.call-start
  61.8 0.0 copy-done.5
  61.8 0.6 fusion.9.slots_ref
  62.4 25.7 %all-to-all-done.x_ref = bf16[128,64,128]{2,1,0:T(8,128)(2,1)S(1)} async-done(((bf16[128,64,128]{2,1,0:T(8,128)(2,1)}), bf16[128,64,128]{2,1,0:T(8,128)(2,1)S(1)}, u32[]{:S(2)}, u32[]{:S(2)}) %all-to-all-start) | async-done | bytes 2097184 | tf_op jit(solution)/shard_map/all_to_all | solution.py:140
  88.1 1.3 copy-done.3
  89.4 41.7 %shard_map.77 = f32[4,8,64,128]{3,2,1,0:T(8,128)} custom-call(s32[192]{0:T(256)} %bitcast.33, s32[192]{0:T(256)} %fusion.9.slots_ref, bf16[192,64,256]{2,1,0:T(8,128)(2,1)} %bitcast.20, bf16[128,64,128]{2,1,0:T(8,128)(2,1)} %copy-done.3), custom_call_target="tpu_custom_call" | custom-call | tf_op jit(solution)/shard_map/pallas_call | solution.py:65
  131.1 0.0 reduce-scatter.5.cloned.1.call-update
  131.2 12.7 %all_gather.14.a_ref = bf16[4,8,64,128]{3,2,1,0:T(8,128)(2,1)} all-gather(bf16[1,8,64,128]{3,2,1,0:T(8,128)(2,1)S(1)} %bitcast.28), channel_id=1, replica_groups=mesh['z'=8,'x'=4,'c'=2,'edge'=4] {'edge'}, dimensions={0}, use_global_device_ids=true | all-gather | bytes 655360 | tf_op jit(solution)/shard_map/all_gather | solution.py:153
  143.9 31.3 %shard_map.79 = f32[128,64,128]{2,1,0:T(8,128)} custom-call(s32[192]{0:T(256)} %bitcast.34, s32[192]{0:T(256)} %fusion.9.slots_ref, bf16[192,64,256]{2,1,0:T(8,128)(2,1)} %bitcast.21, bf16[4,8,64,128]{3,2,1,0:T(8,128)(2,1)} %all_gather.14.a_ref), custom_call_target="tpu_custom_call" | custom-call | tf_op jit(solution)/shard_map/pallas_call | solution.py:86
  175.2 7.9 %all-to-all-start.2 = ((f32[128,64,128]{2,1,0:T(8,128)}), f32[128,64,128]{2,1,0:T(8,128)}, u32[]{:S(2)}, u32[]{:S(2)}) async-start(f32[128,64,128]{2,1,0:T(8,128)} %shard_map.79), calls=%async_computation.4 | async-start | bytes 8388608 | tf_op jit(solution)/shard_map/all_to_all | solution.py:155
  183.1 1.7 add_convert_fusion
  184.8 0.0 all-gather.5.cloned.1.call-update
  184.8 0.0 reduce-scatter.9.cloned.1.call-start
  184.8 0.1 copy.16
  185.0 0.1 copy.17
  185.0 47.0 %all-to-all-done.2 = f32[128,64,128]{2,1,0:T(8,128)} async-done(((f32[128,64,128]{2,1,0:T(8,128)}), f32[128,64,128]{2,1,0:T(8,128)}, u32[]{:S(2)}, u32[]{:S(2)}) %all-to-all-start.2) | async-done | bytes 4194336 | tf_op jit(solution)/shard_map/all_to_all | solution.py:155
  232.0 5.9 %reshape.111 = f32[8,8,2,8192]{3,2,1,0:T(2,128)} reshape(f32[128,64,128]{2,1,0:T(8,128)} %all-to-all-done.2) | data formatting | bytes 8388608 | tf_op jit(solution)/shard_map/reshape | solution.py:158
  237.9 4.6 %copy.18 = f32[8,8,2,8192]{3,2,1,0:T(2,128)} copy(f32[8,8,2,8192]{3,2,0,1:T(2,128)} %bitcast.24) | data formatting | bytes 8388608 | tf_op jit(solution)/shard_map/transpose | solution.py:159
  242.5 6.1 %reshape.112 = f32[8,16,8192]{2,1,0:T(8,128)} reshape(f32[8,8,2,8192]{3,2,1,0:T(2,128)} %copy.18) | data formatting | bytes 8388608 | tf_op jit(solution)/shard_map/reshape | solution.py:159
  248.7 5.0 %fusion.2 = f32[8,8,8192]{2,1,0:T(8,128)} fusion(f32[8,16,8192]{2,1,0:T(8,128)} %reshape.112, s32[8,16]{1,0:T(8,128)S(1)} %copy.17), kind=kOutput, calls=%fused_computation.14 | convolution fusion | flops 100664320 | bytes 6291968 | tf_op jit(solution)/shard_map/zjq,zqd->zjd/dot_general | solution.py:160
  253.7 0.0 reduce-scatter.9.cloned.1.call-update
  253.7 0.0 all-gather.5.cloned.1.call-done
  253.8 2.2 gather_fusion.2
  255.9 1.6 broadcast_select_fusion.1
  257.6 4.4 all-to-all-start.1
  261.9 26.2 %reduce-scatter.9.cloned.1.call-done = f32[1,8,8192]{2,1,0:T(8,128)} async-done(((f32[8,8,8192]{2,1,0:T(8,128)}), f32[1,8,8192]{2,1,0:T(8,128)}) %reduce-scatter.9.cloned.1.call-update) | async-done | bytes 262160 | tf_op jit(solution)/shard_map/reduce_scatter | solution.py:163
  288.2 1.0 broadcast_multiply_fusion.1
  289.2 11.1 %all_gather.15.a_ref = bf16[4,8,64,128]{3,2,1,0:T(8,128)(2,1)} all-gather(bf16[1,8,64,128]{3,2,1,0:T(8,128)(2,1)S(1)} %copy.19), channel_id=1, replica_groups=mesh['z'=8,'x'=4,'c'=2,'edge'=4] {'edge'}, dimensions={0}, use_global_device_ids=true | all-gather | bytes 655360 | tf_op jit(solution)/shard_map/all_gather | solution.py:153
  300.3 31.2 %shard_map.80 = f32[128,64,128]{2,1,0:T(8,128)} custom-call(s32[192]{0:T(256)} %bitcast.35, s32[192]{0:T(256)} %fusion.9.slots_ref, bf16[192,64,256]{2,1,0:T(8,128)(2,1)} %bitcast.22, bf16[4,8,64,128]{3,2,1,0:T(8,128)(2,1)} %all_gather.15.a_ref), custom_call_target="tpu_custom_call" | custom-call | tf_op jit(solution)/shard_map/pallas_call | solution.py:86
  331.5 0.0 all-to-all-done.1.x_ref
  331.5 1.4 copy-done.2
  332.9 12.1 %all-to-all-start.3 = ((f32[128,64,128]{2,1,0:T(8,128)}), f32[128,64,128]{2,1,0:T(8,128)}, u32[]{:S(2)}, u32[]{:S(2)}) async-start(f32[128,64,128]{2,1,0:T(8,128)} %shard_map.80), calls=%async_computation.6 | async-start | bytes 8388608 | tf_op jit(solution)/shard_map/all_to_all | solution.py:155
  345.0 41.6 %shard_map.78 = f32[4,8,64,128]{3,2,1,0:T(8,128)} custom-call(s32[192]{0:T(256)} %bitcast.36, s32[192]{0:T(256)} %fusion.9.slots_ref, bf16[192,64,256]{2,1,0:T(8,128)(2,1)} %bitcast.23, bf16[128,64,128]{2,1,0:T(8,128)(2,1)} %copy-done.2), custom_call_target="tpu_custom_call" | custom-call | tf_op jit(solution)/shard_map/pallas_call | solution.py:65
  386.6 0.0 reduce-scatter.7.cloned.1.call-update
  386.6 0.0 reduce-scatter.11.cloned.1.call-start
  386.7 7.2 %all-to-all-done.3 = f32[128,64,128]{2,1,0:T(8,128)} async-done(((f32[128,64,128]{2,1,0:T(8,128)}), f32[128,64,128]{2,1,0:T(8,128)}, u32[]{:S(2)}, u32[]{:S(2)}) %all-to-all-start.3) | async-done | bytes 4194336 | tf_op jit(solution)/shard_map/all_to_all | solution.py:155
  393.9 5.9 %reshape.113 = f32[8,8,2,8192]{3,2,1,0:T(2,128)} reshape(f32[128,64,128]{2,1,0:T(8,128)} %all-to-all-done.3) | data formatting | bytes 8388608 | tf_op jit(solution)/shard_map/reshape | solution.py:158
  399.8 4.7 %copy.20 = f32[8,8,2,8192]{3,2,1,0:T(2,128)} copy(f32[8,8,2,8192]{3,2,0,1:T(2,128)} %bitcast.25) | data formatting | bytes 8388608 | tf_op jit(solution)/shard_map/transpose | solution.py:159
  404.5 6.1 %reshape.114 = f32[8,16,8192]{2,1,0:T(8,128)} reshape(f32[8,8,2,8192]{3,2,1,0:T(2,128)} %copy.20) | data formatting | bytes 8388608 | tf_op jit(solution)/shard_map/reshape | solution.py:159
  410.6 5.1 %fusion.1 = f32[8,8,8192]{2,1,0:T(8,128)} fusion(f32[8,16,8192]{2,1,0:T(8,128)} %reshape.114, s32[8,16]{1,0:T(8,128)S(1)} %copy.17), kind=kOutput, calls=%fused_computation.13 | convolution fusion | flops 100664320 | bytes 6291968 | tf_op jit(solution)/shard_map/zjq,zqd->zjd/dot_general | solution.py:160
  415.7 0.0 reduce-scatter.11.cloned.1.call-update
  415.7 0.0 copy-start.1
  415.7 0.0 reduce-scatter.7.cloned.1.call-done
  415.8 1.7 multiply_add_fusion
  417.5 33.7 %reduce-scatter.11.cloned.1.call-done = f32[1,8,8192]{2,1,0:T(8,128)} async-done(((f32[8,8,8192]{2,1,0:T(8,128)}), f32[1,8,8192]{2,1,0:T(8,128)}) %reduce-scatter.11.cloned.1.call-update) | async-done | bytes 262160 | tf_op jit(solution)/shard_map/reduce_scatter | solution.py:163
  451.1 1.0 broadcast_multiply_fusion
  452.2 0.7 add_add_fusion
  452.9 0.0 copy-done.1
  (20 shorter events, 0.2 us)
Async XLA Ops:
  7.2 2.0 copy-start
  7.2 40.7 %all-gather.3.cloned.1.call-start = ((), (), s32[]{:S(2)}) async-start(), calls=%async_computation.8 | async-start | bytes 1179648 | tf_op jit(solution)/shard_map/all_gather | solution.py:138
  51.6 10.2 %copy-start.5 = (f32[512,128]{1,0:T(8,128)S(1)}, f32[512,128]{1,0:T(8,128)}, u32[]{:S(2)}) copy-start(f32[512,128]{1,0:T(8,128)} %param.9) | copy-start | bytes 786436
  51.6 10.2 %copy-start.6 = (s32[1,192]{1,0:T(1,128)S(1)}, s32[1,192]{1,0:T(1,128)}, u32[]{:S(2)}) copy-start(s32[1,192]{1,0:T(1,128)} %param.12) | copy-start | bytes 2308
  51.6 36.5 %all-to-all-start = ((bf16[128,64,128]{2,1,0:T(8,128)(2,1)}), bf16[128,64,128]{2,1,0:T(8,128)(2,1)S(1)}, u32[]{:S(2)}, u32[]{:S(2)}) async-start(bf16[128,64,128]{2,1,0:T(8,128)(2,1)} %broadcast_select_fusion), calls=%async_computation | async-start | bytes 4194304 | tf_op jit(solution)/shard_map/all_to_all | solution.py:140
  61.8 121.3 %reduce-scatter.5.cloned.1.call-start = ((), (), s32[]{:S(2)}) async-start(), calls=%async_computation.9 | async-start | bytes 1310720 | tf_op jit(solution)/shard_map/reduce_scatter | solution.py:144
  88.1 1.3 copy-start.3
  175.2 7.9 %copy-start.4 = (f32[512,128]{1,0:T(8,128)S(1)}, f32[512,128]{1,0:T(8,128)}, u32[]{:S(2)}) copy-start(f32[512,128]{1,0:T(8,128)} %param.8) | copy-start | bytes 786436
  175.2 56.9 %all-to-all-start.2 = ((f32[128,64,128]{2,1,0:T(8,128)}), f32[128,64,128]{2,1,0:T(8,128)}, u32[]{:S(2)}, u32[]{:S(2)}) async-start(f32[128,64,128]{2,1,0:T(8,128)} %shard_map.79), calls=%async_computation.4 | async-start | bytes 8388608 | tf_op jit(solution)/shard_map/all_to_all | solution.py:155
  183.1 70.6 %all-gather.5.cloned.1.call-start = ((), (), s32[]{:S(2)}) async-start(), calls=%async_computation.10 | async-start | bytes 1179648 | tf_op jit(solution)/shard_map/all_gather | solution.py:138
  184.8 103.4 %reduce-scatter.9.cloned.1.call-start = ((), (), s32[]{:S(2)}) async-start(), calls=%async_computation.12 | async-start | bytes 2359296 | tf_op jit(solution)/shard_map/reduce_scatter | solution.py:163
  257.6 73.9 %all-to-all-start.1 = ((bf16[128,64,128]{2,1,0:T(8,128)(2,1)}), bf16[128,64,128]{2,1,0:T(8,128)(2,1)S(1)}, u32[]{:S(2)}, u32[]{:S(2)}) async-start(bf16[128,64,128]{2,1,0:T(8,128)(2,1)} %broadcast_select_fusion.1), calls=%async_computation.2 | async-start | bytes 4194304 | tf_op jit(solution)/shard_map/all_to_all | solution.py:140
  331.5 1.4 copy-start.2
  332.9 61.0 %all-to-all-start.3 = ((f32[128,64,128]{2,1,0:T(8,128)}), f32[128,64,128]{2,1,0:T(8,128)}, u32[]{:S(2)}, u32[]{:S(2)}) async-start(f32[128,64,128]{2,1,0:T(8,128)} %shard_map.80), calls=%async_computation.6 | async-start | bytes 8388608 | tf_op jit(solution)/shard_map/all_to_all | solution.py:155
  345.0 70.8 %reduce-scatter.7.cloned.1.call-start = ((), (), s32[]{:S(2)}) async-start(), calls=%async_computation.11 | async-start | bytes 1310720 | tf_op jit(solution)/shard_map/reduce_scatter | solution.py:144
  386.6 64.5 %reduce-scatter.11.cloned.1.call-start = ((), (), s32[]{:S(2)}) async-start(), calls=%async_computation.13 | async-start | bytes 2359296 | tf_op jit(solution)/shard_map/reduce_scatter | solution.py:163
  415.7 37.2 %copy-start.1 = (s32[64,128]{1,0:T(8,128)S(1)}, s32[64,128]{1,0:T(8,128)}, u32[]{:S(2)}) copy-start(s32[64,128]{1,0:T(8,128)} %param.10) | copy-start | bytes 98308
Sparse Core Ops, SparseCore 0:
  10.4 37.4 all-gather.2
  131.3 22.6 reduce-scatter.4
  186.4 32.3 all-gather.4
  253.9 34.2 reduce-scatter.8
  386.7 22.9 reduce-scatter.6
  415.8 35.2 reduce-scatter.10

commit v2 on v1

--- a/solution.py
+++ b/solution.py
@@ -1,5 +1,3 @@
-import functools
-
 import jax
 import jax.numpy as jnp
 from jax import lax
@@ -13,10 +11,11 @@
 Z_SIZE = 8
 X_SIZE = 4
 CORE_SIZE = 2
-CHUNK = 16
-
-
-def forward_kernel(rows_ref, slots_ref, v_ref, x_ref, out_ref):
+GROUP = 4
+GROUPS_PER_STEP = 8
+
+
+def forward_kernel(rows_ref, slots_ref, vt_ref, x_ref, out_ref):
     step = pl.program_id(0)
 
     @pl.when(step == 0)
@@ -26,16 +25,16 @@
     quarters, _, quarter, hidden = out_ref.shape
 
     def body(i, carry):
-        b = step * CHUNK + i
-        j = rows_ref[b]
-        s = slots_ref[b]
-        product = lax.dot_general(
-            v_ref[i], x_ref[s], (((0,), (0,)), ((), ())), preferred_element_type=jnp.float32
-        )
+        g = step * GROUPS_PER_STEP + i
+        j = rows_ref[g]
+        sources = jnp.concatenate(
+            [x_ref[slots_ref[g * GROUP + m]] for m in range(GROUP)], axis=0
+        )
+        product = jnp.dot(vt_ref[i], sources, preferred_element_type=jnp.float32)
         out_ref[:, j] += product.reshape(quarters, quarter, hidden)
         return carry
 
-    lax.fori_loop(0, CHUNK, body, 0)
+    lax.fori_loop(0, GROUPS_PER_STEP, body, 0)
 
 
 def backward_kernel(rows_ref, slots_ref, v_ref, a_ref, out_ref):
@@ -48,28 +47,45 @@
     quarters, _, quarter, hidden = a_ref.shape
 
     def body(i, carry):
-        b = step * CHUNK + i
-        j = rows_ref[b]
-        s = slots_ref[b]
+        g = step * GROUPS_PER_STEP + i
+        j = rows_ref[g]
         sources = a_ref[:, j].reshape(quarters * quarter, hidden)
-        out_ref[s] += jnp.dot(v_ref[i], sources, preferred_element_type=jnp.float32)
+        product = jnp.dot(v_ref[i], sources, preferred_element_type=jnp.float32)
+        for m in range(GROUP):
+            s = slots_ref[g * GROUP + m]
+            out_ref[s] += product[m * quarter:(m + 1) * quarter]
         return carry
 
-    lax.fori_loop(0, CHUNK, body, 0)
-
-
-def forward_apply(rows, slots, weights, received, quarters):
-    block_count, quarter, width = weights.shape
-    hidden = received.shape[-1]
-    blocks_dev = 8
+    lax.fori_loop(0, GROUPS_PER_STEP, body, 0)
+
+
+def combine_kernel(want_ref, arrived_ref, out_ref):
+    out_ref[...] = jnp.zeros_like(out_ref)
+    lines = out_ref.shape[0]
+
+    def body(q, carry):
+        j = want_ref[q]
+
+        @pl.when(j >= 0)
+        def _():
+            out_ref[q // CAP % lines, j] += arrived_ref[q]
+
+        return carry
+
+    lax.fori_loop(0, arrived_ref.shape[0], body, 0)
+
+
+def forward_apply(rows, slots, weights_t, received, quarters, blocks_dev):
+    group_count, width, depth = weights_t.shape
+    quarter, hidden = received.shape[1:]
     return pl.pallas_call(
         forward_kernel,
         out_shape=jax.ShapeDtypeStruct((quarters, blocks_dev, quarter, hidden), jnp.float32),
         grid_spec=pltpu.PrefetchScalarGridSpec(
             num_scalar_prefetch=2,
-            grid=(block_count // CHUNK,),
+            grid=(group_count // GROUPS_PER_STEP,),
             in_specs=[
-                pl.BlockSpec((CHUNK, quarter, width), lambda i, r, s: (i, 0, 0)),
+                pl.BlockSpec((GROUPS_PER_STEP, width, depth), lambda i, r, s: (i, 0, 0)),
                 pl.BlockSpec(received.shape, lambda i, r, s: (0, 0, 0)),
             ],
             out_specs=pl.BlockSpec(
@@ -77,26 +93,65 @@
             ),
         ),
         compiler_params=pltpu.CompilerParams(dimension_semantics=("arbitrary",)),
-    )(rows, slots, weights, received)
-
-
-def backward_apply(rows, slots, weights, sources, slot_total):
-    block_count, quarter, width = weights.shape
-    hidden = sources.shape[-1]
+    )(rows, slots, weights_t, received)
+
+
+def backward_apply(rows, slots, weights_g, sources, slot_total):
+    group_count, depth, width = weights_g.shape
+    quarter, hidden = sources.shape[2:]
     return pl.pallas_call(
         backward_kernel,
         out_shape=jax.ShapeDtypeStruct((slot_total, quarter, hidden), jnp.float32),
         grid_spec=pltpu.PrefetchScalarGridSpec(
             num_scalar_prefetch=2,
-            grid=(block_count // CHUNK,),
+            grid=(group_count // GROUPS_PER_STEP,),
             in_specs=[
-                pl.BlockSpec((CHUNK, quarter, width), lambda i, r, s: (i, 0, 0)),
+                pl.BlockSpec((GROUPS_PER_STEP, depth, width), lambda i, r, s: (i, 0, 0)),
                 pl.BlockSpec(sources.shape, lambda i, r, s: (0, 0, 0, 0)),
             ],
             out_specs=pl.BlockSpec((slot_total, quarter, hidden), lambda i, r, s: (0, 0, 0)),
         ),
         compiler_params=pltpu.CompilerParams(dimension_semantics=("arbitrary",)),
-    )(rows, slots, weights, sources)
+    )(rows, slots, weights_g, sources)
+
+
+def combine_apply(wanted, arrived, blocks_dev):
+    slot_total, quarter, hidden = arrived.shape
+    lines = slot_total // (CAP * X_SIZE * CORE_SIZE)
+    return pl.pallas_call(
+        combine_kernel,
+        out_shape=jax.ShapeDtypeStruct((lines, blocks_dev, quarter, hidden), jnp.float32),
+        grid_spec=pltpu.PrefetchScalarGridSpec(
+            num_scalar_prefetch=1,
+            grid=(1,),
+            in_specs=[pl.BlockSpec(arrived.shape, lambda i, w: (0, 0, 0))],
+            out_specs=pl.BlockSpec(
+                (lines, blocks_dev, quarter, hidden), lambda i, w: (0, 0, 0, 0)
+            ),
+        ),
+    )(wanted, arrived)
+
+
+def grouping(row_ids, blocks_dev):
+    block_count = row_ids.shape[0]
+    group_count = block_count // GROUP + blocks_dev
+    order = jnp.argsort(row_ids, stable=True).astype(jnp.int32)
+    sorted_rows = row_ids[order]
+    counts = jnp.sum(
+        (row_ids[None, :] == jnp.arange(blocks_dev, dtype=jnp.int32)[:, None]).astype(jnp.int32), axis=1
+    )
+    groups_per_row = (counts + GROUP - 1) // GROUP
+    group_end = jnp.cumsum(groups_per_row)
+    group_start = group_end - groups_per_row
+    row_start = jnp.cumsum(counts) - counts
+    rank = jnp.arange(block_count, dtype=jnp.int32) - row_start[sorted_rows]
+    position = group_start[sorted_rows] * GROUP + rank
+    member = jnp.full((group_count * GROUP,), block_count, jnp.int32).at[position].set(order)
+    group_range = jnp.arange(group_count, dtype=jnp.int32)
+    group_row = jnp.minimum(
+        jnp.sum((group_range[:, None] >= group_end[None, :]).astype(jnp.int32), axis=1), blocks_dev - 1
+    ).astype(jnp.int32)
+    return member, group_row
 
 
 def per_device(teleport, cotangent, fetch_table, block_row, block_slot, values):
@@ -127,10 +182,19 @@
     table_cols = line_owners[:, None] * CAP + jnp.arange(CAP, dtype=jnp.int32)[None, :]
     wanted = fetch_table[peer_groups[:, None, None], table_cols[None, :, :]]
     send_index = (z_range[None, :, None] * blocks_dev + jnp.maximum(wanted, 0)).reshape(-1)
-    wanted_hot = (
-        wanted.transpose(1, 0, 2).reshape(Z_SIZE, 1, row_peers * CAP)
-        == jnp.arange(blocks_dev, dtype=jnp.int32)[None, :, None]
-    ).astype(jnp.float32)
+
+    member, group_row = grouping(row_ids, blocks_dev)
+    member_slot = jnp.concatenate([placed_slots, jnp.zeros((1,), jnp.int32)])[member]
+    padded = jnp.concatenate([weights, jnp.zeros((1,) + weights.shape[1:], weights.dtype)])[member]
+    group_count = member.shape[0] // GROUP
+    width = weights.shape[2]
+    weights_g = padded.reshape(group_count, GROUP * quarter, width)
+    weights_t = (
+        padded.reshape(group_count, GROUP, quarter, width)
+        .transpose(0, 3, 1, 2)
+        .reshape(group_count, width, GROUP * quarter)
+    )
+    wanted_flat = wanted.reshape(-1)
 
     current = teleport
     for step_index in range(STEPS):
@@ -140,7 +204,7 @@
         received = lax.all_to_all(
             outgoing, ("x", "c"), split_axis=0, concat_axis=0, tiled=True
         )
-        partial = forward_apply(row_ids, placed_slots, weights, received, quarters)
+        partial = forward_apply(group_row, member_slot, weights_t, received, quarters, blocks_dev)
         summed = lax.psum_scatter(
             partial.reshape(quarters * row_count, hidden), "edge", scatter_dimension=0, tiled=True
         )
@@ -151,15 +215,11 @@
     for step_index in range(STEPS):
         rounded = adjoint.astype(jnp.bfloat16).reshape(1, blocks_dev, quarter, hidden)
         whole_rows = lax.all_gather(rounded, "edge", axis=0, tiled=True)
-        slot_sums = backward_apply(row_ids, placed_slots, weights, whole_rows, slot_total)
+        slot_sums = backward_apply(group_row, member_slot, weights_g, whole_rows, slot_total)
         arrived = lax.all_to_all(
             slot_sums, ("x", "c"), split_axis=0, concat_axis=0, tiled=True
         )
-        arrived = arrived.reshape(row_peers, Z_SIZE, CAP, quarter * hidden)
-        arrived = arrived.transpose(1, 0, 2, 3).reshape(Z_SIZE, row_peers * CAP, quarter * hidden)
-        dense = jnp.einsum(
-            "zjq,zqd->zjd", wanted_hot, arrived, precision=lax.Precision.HIGHEST
-        )
+        dense = combine_apply(wanted_flat, arrived, blocks_dev)
         owned = lax.psum_scatter(dense, "z", scatter_dimension=0, tiled=True)
         adjoint = 0.9 * owned.reshape(row_count, hidden)
         factor = 0.1 if step_index + 1 < STEPS else 1.0

time: 464 us -> 390 us (0.84)
  Pallas kernels: 146 us -> 71.3 us
  other arithmetic: 11.8 us -> 26.8 us
  matrix products: 10.1 us -> 0 us
  waiting for transfers between devices: 177 us -> 172 us
    pallas_call x2, Pallas kernels: 83.3 us -> 27.5 us  [forward_apply(): pl.pallas_call(forward_kernel, out_shape=jax.ShapeDtypeStruct((quarters,...]
    pallas_call x2, Pallas kernels: 62.5 us -> 29.8 us  [backward_apply(): pl.pallas_call(backward_kernel, out_shape=jax.ShapeDtypeStruct((slot_tota...]
    all_to_all x2, waiting for transfers between devices: 54.2 us -> 82.3 us  [per_device(): lax.all_to_all(slot_sums, ('x', 'c'), split_axis=0, concat_axis=0, tiled=...]
    all_to_all x2, waiting for transfers between devices: 25.7 us -> 0.01 us  [per_device(): lax.all_to_all(outgoing, ('x', 'c'), split_axis=0, concat_axis=0, tiled=T...]
    gather x0 -> x4, local copies, waits for them, and re-layouts: none -> 16.4 us  [the longest x1 11.2 us: per_device(): jnp.concatenate([weights, jnp.zeros((1,) + weights.shape[1:], weights.dty...]
    pallas_call x0 -> x2, Pallas kernels: none -> 14 us  [combine_apply(): pl.pallas_call(combine_kernel, out_shape=jax.ShapeDtypeStruct((lines, blo...]
    reshape x4 -> x1, local copies, waits for them, and re-layouts: 24 us -> 10.4 us  [per_device(): weights_t = padded.reshape(group_count, GROUP, quarter, width).transpose(...]
    dot_general x2 -> x0, matrix products: 10.1 us -> none  [per_device(): jnp.einsum('zjq,zqd->zjd', wanted_hot, arrived, precision=lax.Precision.H...]
  transfers between devices with their start and end apart: 10 -> 10, of which waited for: 6 -> 5; matrix products, arithmetic and copies ran while one was open for 12% -> 16% of each run, Pallas kernels for 23% -> 15%
where the time goes in v2:
time: 390 us; the launch traced here: 386 us
  waiting for transfers between devices  172 us (44%)
  Pallas kernels  71.3 us (18%)
  local copies, waits for them, and re-layouts  43.3 us (11%)
  starting transfers between devices  35.1 us (9%)
  other arithmetic  26.8 us (7%)
  blocking collectives  22.7 us (6%)
  between operations  14.3 us (4%)
    all_to_all x2, waiting for transfers between devices, per_device(): lax.all_to_all(slot_sums, ('x', 'c'), split_axis=0, concat_axis=0, tiled=...  82.3 us
    reduce_scatter x2, waiting for transfers between devices, per_device(): owned = lax.psum_scatter(dense, 'z', scatter_dimension=0, tiled=True)  59.6 us
    all_gather x2, waiting for transfers between devices, per_device(): line_blocks = lax.all_gather(rounded, 'z', axis=0, tiled=True)  30.1 us
    pallas_call x2, Pallas kernels, backward_apply(): pl.pallas_call(backward_kernel, out_shape=jax.ShapeDtypeStruct((slot_tota...  29.8 us
    pallas_call x2, Pallas kernels, forward_apply(): pl.pallas_call(forward_kernel, out_shape=jax.ShapeDtypeStruct((quarters,...  27.5 us
    all_gather x2, blocking collectives, per_device(): whole_rows = lax.all_gather(rounded, 'edge', axis=0, tiled=True)  22.7 us
    all_to_all x2, starting transfers between devices, per_device(): lax.all_to_all(slot_sums, ('x', 'c'), split_axis=0, concat_axis=0, tiled=...  20.5 us
    all_to_all x2, starting transfers between devices, per_device(): lax.all_to_all(outgoing, ('x', 'c'), split_axis=0, concat_axis=0, tiled=T...  14.5 us
  transfers between devices with their start and end apart: 10, of which 5 were waited for; matrix products, arithmetic and copies ran while one was open for 16% of the time, Pallas kernels for 15%

profile of v2, /device:TPU:1, one launch (start us, length us, event | category | flops | bytes accessed | tf_op | source)
XLA Modules:
  0.0 385.6 jit_solution(1967084386509825566)
XLA Ops:
  7.2 0.0 copy-start
  7.2 0.0 all-gather.3.cloned.1.call-start
  7.2 1.6 convert_element_type.21
  8.8 0.0 all-gather.3.cloned.1.call-update
  8.9 0.8 convert_reduce_fusion
  9.7 0.2 reduce-window.17
  9.9 0.2 reduce-window.18
  10.1 3.8 sort.17
  13.9 2.0 gather_fusion
  15.9 0.1 fusion.1
  16.0 0.1 broadcast_or_fusion
  16.1 0.1 reshape.302
  16.2 0.1 add.222
  16.3 0.1 add.223
  16.4 1.2 gather_fusion.3
  17.8 30.1 %all-gather.3.cloned.1.call-done = bf16[64,64,128]{2,1,0:T(8,128)(2,1)} async-done(((bf16[8,64,128]{2,1,0:T(8,128)(2,1)}), bf16[64,64,128]{2,1,0:T(8,128)(2,1)}) %all-gather.3.cloned.1.call-update) | async-done | bytes 1048592 | tf_op jit(solution)/shard_map/all_gather | solution.py:202
  47.8 2.2 gather_fusion.4
  50.0 1.6 broadcast_select_fusion
  51.6 10.0 %all-to-all-start = ((bf16[128,64,128]{2,1,0:T(8,128)(2,1)}), bf16[128,64,128]{2,1,0:T(8,128)(2,1)S(1)}, u32[]{:S(2)}, u32[]{:S(2)}) async-start(bf16[128,64,128]{2,1,0:T(8,128)(2,1)} %broadcast_select_fusion), calls=%async_computation | async-start | bytes 4194304 | tf_op jit(solution)/shard_map/all_to_all | solution.py:204
  61.7 0.7 fusion.14
  62.4 8.7 %compare_select_fusion.8 = (s32[192,1]{0,1:T(1,128)S(1)}, s32[192,1]{0,1:T(1,128)S(1)}) fusion(s32[]{:T(128)} %bitcast.17, s32[]{:T(128)} %bitcast.18, s32[]{:T(128)} %bitcast.19, s32[]{:T(128)} %bitcast.20, s32[]{:T(128)} %bitcast.21, s32[]{:T(128)} %bitcast.23, s32[]{:T(128)} %bitcast.22, s32[192,1]{0,1:T(1,128)S(1)} %bitcast.69, s32[]{:T(128)} %bitcast.12, ...), kind=kLoop, calls=%fused_computation.35 | loop fusion | flops 4032 | bytes 2360 | tf_op jit(solution)/shard_map/gather | solution.py:147
  71.0 1.3 broadcast_select_fusion.2
  72.3 1.2 scatter_custom_fusion
  73.5 6.6 %concatenate.10 = bf16[193,64,256]{2,1,0:T(8,128)(2,1)} pad(bf16[192,64,256]{2,1,0:T(8,128)(2,1)} %bitcast.58, bf16[]{:T(256)} %constant.145.clone.1), padding=0_1x0_0x0_0 | pad | bytes 12615682 | tf_op jit(solution)/shard_map/concatenate | solution.py:188
  80.1 0.0 copy-start.7
  80.1 11.2 %gather_fusion.2 = bf16[224,64,256]{2,1,0:T(8,128)(2,1)} fusion(bf16[193,64,256]{2,1,0:T(8,128)(2,1)} %concatenate.10, s32[1024]{0:T(1024)S(1)} %pad_clamp_fusion.1), kind=kCustom, calls=%fused_computation.4 | custom fusion | bytes 14680960 | tf_op jit(solution)/shard_map/gather | solution.py:188
  91.4 0.1 pad_add_fusion
  91.5 2.5 gather_fusion.1
  94.0 10.4 %copy.14.vt_ref = bf16[56,256,256]{2,1,0:T(8,128)(2,1)} copy(bf16[56,256,256]{1,2,0:T(8,128)(2,1)} %bitcast.55) | data formatting | bytes 14680064 | tf_op jit(solution)/shard_map/reshape | solution.py:195
  104.4 0.1 convert_reduce_fusion.1
  104.4 0.6 broadcast_minimum_fusion.rows_ref
  105.0 1.3 copy-done.2
  106.3 13.7 %shard_map.77 = f32[4,8,64,128]{3,2,1,0:T(8,128)} custom-call(s32[56]{0:T(128)} %broadcast_minimum_fusion.rows_ref, s32[224]{0:T(256)} %gather_fusion.1, bf16[56,256,256]{2,1,0:T(8,128)(2,1)} %copy.14.vt_ref, bf16[128,64,128]{2,1,0:T(8,128)(2,1)} %copy-done.2), custom_call_target="tpu_custom_call" | custom-call | tf_op jit(solution)/shard_map/pallas_call | solution.py:81
  120.1 0.0 reduce-scatter.5.cloned.1.call-update
  120.1 11.5 %all_gather.14.a_ref = bf16[4,8,64,128]{3,2,1,0:T(8,128)(2,1)} all-gather(bf16[1,8,64,128]{3,2,1,0:T(8,128)(2,1)S(1)} %bitcast.61), channel_id=1, replica_groups=mesh['z'=8,'x'=4,'c'=2,'edge'=4] {'edge'}, dimensions={0}, use_global_device_ids=true | all-gather | bytes 655360 | tf_op jit(solution)/shard_map/all_gather | solution.py:217
  131.7 14.9 %shard_map.79 = f32[128,64,128]{2,1,0:T(8,128)} custom-call(s32[56]{0:T(128)} %broadcast_minimum_fusion.rows_ref, s32[224]{0:T(256)} %gather_fusion.1, bf16[56,256,256]{2,1,0:T(8,128)(2,1)} %bitcast.56, bf16[4,8,64,128]{3,2,1,0:T(8,128)(2,1)} %all_gather.14.a_ref), custom_call_target="tpu_custom_call" | custom-call | tf_op jit(solution)/shard_map/pallas_call | solution.py:102
  146.6 8.5 %all-to-all-start.2 = ((f32[128,64,128]{2,1,0:T(8,128)}), f32[128,64,128]{2,1,0:T(8,128)}, u32[]{:S(2)}, u32[]{:S(2)}) async-start(f32[128,64,128]{2,1,0:T(8,128)} %shard_map.79), calls=%async_computation.4 | async-start | bytes 8388608 | tf_op jit(solution)/shard_map/all_to_all | solution.py:219
  155.1 1.7 add_convert_fusion
  156.7 0.0 all-gather.5.cloned.1.call-update
  156.8 0.0 reduce-scatter.9.cloned.1.call-start
  156.8 47.2 %all-to-all-done.2.arrived_ref = f32[128,64,128]{2,1,0:T(8,128)} async-done(((f32[128,64,128]{2,1,0:T(8,128)}), f32[128,64,128]{2,1,0:T(8,128)}, u32[]{:S(2)}, u32[]{:S(2)}) %all-to-all-start.2) | async-done | bytes 4194336 | tf_op jit(solution)/shard_map/all_to_all | solution.py:219
  204.0 7.0 %shard_map.80 = f32[8,8,64,128]{3,2,1,0:T(8,128)} custom-call(s32[128]{0:T(128)} %copy-done.5, f32[128,64,128]{2,1,0:T(8,128)} %all-to-all-done.2.arrived_ref), custom_call_target="tpu_custom_call" | custom-call | tf_op jit(solution)/shard_map/pallas_call | solution.py:121
  211.0 0.0 reduce-scatter.9.cloned.1.call-update
  211.0 0.0 all-gather.5.cloned.1.call-done
  211.0 2.2 gather_fusion.5
  213.2 1.6 broadcast_select_fusion.1
  214.8 4.5 %all-to-all-start.1 = ((bf16[128,64,128]{2,1,0:T(8,128)(2,1)}), bf16[128,64,128]{2,1,0:T(8,128)(2,1)S(1)}, u32[]{:S(2)}, u32[]{:S(2)}) async-start(bf16[128,64,128]{2,1,0:T(8,128)(2,1)} %broadcast_select_fusion.1), calls=%async_computation.2 | async-start | bytes 4194304 | tf_op jit(solution)/shard_map/all_to_all | solution.py:204
  219.2 26.1 %reduce-scatter.9.cloned.1.call-done = f32[1,8,64,128]{3,2,1,0:T(8,128)} async-done(((f32[8,8,64,128]{3,2,1,0:T(8,128)}), f32[1,8,64,128]{3,2,1,0:T(8,128)}) %reduce-scatter.9.cloned.1.call-update) | async-done | bytes 262160 | tf_op jit(solution)/shard_map/reduce_scatter | solution.py:223
  245.4 1.0 broadcast_multiply_fusion.1
  246.4 11.2 %all_gather.15.a_ref = bf16[4,8,64,128]{3,2,1,0:T(8,128)(2,1)} all-gather(bf16[1,8,64,128]{3,2,1,0:T(8,128)(2,1)S(1)} %get-tuple-element.8), channel_id=1, replica_groups=mesh['z'=8,'x'=4,'c'=2,'edge'=4] {'edge'}, dimensions={0}, use_global_device_ids=true | all-gather | bytes 655360 | tf_op jit(solution)/shard_map/all_gather | solution.py:217
  257.5 14.9 %shard_map.81 = f32[128,64,128]{2,1,0:T(8,128)} custom-call(s32[56]{0:T(128)} %broadcast_minimum_fusion.rows_ref, s32[224]{0:T(256)} %gather_fusion.1, bf16[56,256,256]{2,1,0:T(8,128)(2,1)} %bitcast.57, bf16[4,8,64,128]{3,2,1,0:T(8,128)(2,1)} %all_gather.15.a_ref), custom_call_target="tpu_custom_call" | custom-call | tf_op jit(solution)/shard_map/pallas_call | solution.py:102
  272.4 1.4 copy-done.3
  273.8 12.0 %all-to-all-start.3 = ((f32[128,64,128]{2,1,0:T(8,128)}), f32[128,64,128]{2,1,0:T(8,128)}, u32[]{:S(2)}, u32[]{:S(2)}) async-start(f32[128,64,128]{2,1,0:T(8,128)} %shard_map.81), calls=%async_computation.6 | async-start | bytes 8388608 | tf_op jit(solution)/shard_map/all_to_all | solution.py:219
  285.9 13.7 %shard_map.78 = f32[4,8,64,128]{3,2,1,0:T(8,128)} custom-call(s32[56]{0:T(128)} %broadcast_minimum_fusion.rows_ref, s32[224]{0:T(256)} %gather_fusion.1, bf16[56,256,256]{2,1,0:T(8,128)(2,1)} %copy.14.vt_ref, bf16[128,64,128]{2,1,0:T(8,128)(2,1)} %copy-done.3), custom_call_target="tpu_custom_call" | custom-call | tf_op jit(solution)/shard_map/pallas_call | solution.py:81
  299.6 0.0 reduce-scatter.7.cloned.1.call-update
  299.6 0.0 reduce-scatter.11.cloned.1.call-start
  299.7 35.1 %all-to-all-done.3.arrived_ref = f32[128,64,128]{2,1,0:T(8,128)} async-done(((f32[128,64,128]{2,1,0:T(8,128)}), f32[128,64,128]{2,1,0:T(8,128)}, u32[]{:S(2)}, u32[]{:S(2)}) %all-to-all-start.3) | async-done | bytes 4194336 | tf_op jit(solution)/shard_map/all_to_all | solution.py:219
  334.8 7.0 %shard_map.82 = f32[8,8,64,128]{3,2,1,0:T(8,128)} custom-call(s32[128]{0:T(128)} %copy-done.5, f32[128,64,128]{2,1,0:T(8,128)} %all-to-all-done.3.arrived_ref), custom_call_target="tpu_custom_call" | custom-call | tf_op jit(solution)/shard_map/pallas_call | solution.py:121
  341.8 0.0 reduce-scatter.11.cloned.1.call-update
  341.8 0.0 reduce-scatter.7.cloned.1.call-done
  341.8 1.7 multiply_add_fusion
  343.5 33.5 %reduce-scatter.11.cloned.1.call-done = f32[1,8,64,128]{3,2,1,0:T(8,128)} async-done(((f32[8,8,64,128]{3,2,1,0:T(8,128)}), f32[1,8,64,128]{3,2,1,0:T(8,128)}) %reduce-scatter.11.cloned.1.call-update) | async-done | bytes 262160 | tf_op jit(solution)/shard_map/reduce_scatter | solution.py:223
  377.0 1.0 broadcast_multiply_fusion
  378.0 0.8 bitcast_add_fusion
  (34 shorter events, 0.2 us)
Async XLA Ops:
  7.2 9.3 %copy-start = (s32[64,128]{1,0:T(8,128)S(1)}, s32[64,128]{1,0:T(8,128)}, u32[]{:S(2)}) copy-start(s32[64,128]{1,0:T(8,128)} %param.10) | copy-start | bytes 98308
  7.2 40.7 %all-gather.3.cloned.1.call-start = ((), (), s32[]{:S(2)}) async-start(), calls=%async_computation.8 | async-start | bytes 1179648 | tf_op jit(solution)/shard_map/all_gather | solution.py:202
  17.7 32.3 %copy-start.5 = (s32[128]{0:T(128)}, s32[128]{0:T(128)S(1)}, u32[]{:S(2)}) copy-start(s32[128]{0:T(128)S(1)} %gather_fusion.3) | copy-start | bytes 1540
  51.6 53.4 %all-to-all-start = ((bf16[128,64,128]{2,1,0:T(8,128)(2,1)}), bf16[128,64,128]{2,1,0:T(8,128)(2,1)S(1)}, u32[]{:S(2)}, u32[]{:S(2)}) async-start(bf16[128,64,128]{2,1,0:T(8,128)(2,1)} %broadcast_select_fusion), calls=%async_computation | async-start | bytes 4194304 | tf_op jit(solution)/shard_map/all_to_all | solution.py:204
  61.6 93.4 %reduce-scatter.5.cloned.1.call-start = ((), (), s32[]{:S(2)}) async-start(), calls=%async_computation.9 | async-start | bytes 1310720 | tf_op jit(solution)/shard_map/reduce_scatter | solution.py:208
  80.1 11.2 %copy-start.7 = (s32[1,192]{1,0:T(1,128)S(1)}, s32[1,192]{1,0:T(1,128)}, u32[]{:S(2)}) copy-start(s32[1,192]{1,0:T(1,128)} %param.12) | copy-start | bytes 2308
  105.0 15.1 %copy-start.6 = (f32[512,128]{1,0:T(8,128)S(1)}, f32[512,128]{1,0:T(8,128)}, u32[]{:S(2)}) copy-start(f32[512,128]{1,0:T(8,128)} %param.9) | copy-start | bytes 786436
  105.0 1.3 copy-start.2
  146.6 8.5 %copy-start.4 = (f32[512,128]{1,0:T(8,128)S(1)}, f32[512,128]{1,0:T(8,128)}, u32[]{:S(2)}) copy-start(f32[512,128]{1,0:T(8,128)} %param.8) | copy-start | bytes 786436
  146.6 57.4 %all-to-all-start.2 = ((f32[128,64,128]{2,1,0:T(8,128)}), f32[128,64,128]{2,1,0:T(8,128)}, u32[]{:S(2)}, u32[]{:S(2)}) async-start(f32[128,64,128]{2,1,0:T(8,128)} %shard_map.79), calls=%async_computation.4 | async-start | bytes 8388608 | tf_op jit(solution)/shard_map/all_to_all | solution.py:219
  155.1 55.9 %all-gather.5.cloned.1.call-start = ((), (), s32[]{:S(2)}) async-start(), calls=%async_computation.10 | async-start | bytes 1179648 | tf_op jit(solution)/shard_map/all_gather | solution.py:202
  156.8 88.6 %reduce-scatter.9.cloned.1.call-start = ((), (), s32[]{:S(2)}) async-start(), calls=%async_computation.12 | async-start | bytes 2359296 | tf_op jit(solution)/shard_map/reduce_scatter | solution.py:223
  214.8 57.6 %all-to-all-start.1 = ((bf16[128,64,128]{2,1,0:T(8,128)(2,1)}), bf16[128,64,128]{2,1,0:T(8,128)(2,1)S(1)}, u32[]{:S(2)}, u32[]{:S(2)}) async-start(bf16[128,64,128]{2,1,0:T(8,128)(2,1)} %broadcast_select_fusion.1), calls=%async_computation.2 | async-start | bytes 4194304 | tf_op jit(solution)/shard_map/all_to_all | solution.py:204
  272.4 1.4 copy-start.3
  273.8 61.0 %all-to-all-start.3 = ((f32[128,64,128]{2,1,0:T(8,128)}), f32[128,64,128]{2,1,0:T(8,128)}, u32[]{:S(2)}, u32[]{:S(2)}) async-start(f32[128,64,128]{2,1,0:T(8,128)} %shard_map.81), calls=%async_computation.6 | async-start | bytes 8388608 | tf_op jit(solution)/shard_map/all_to_all | solution.py:219
  285.9 56.0 %reduce-scatter.7.cloned.1.call-start = ((), (), s32[]{:S(2)}) async-start(), calls=%async_computation.11 | async-start | bytes 1310720 | tf_op jit(solution)/shard_map/reduce_scatter | solution.py:208
  299.6 77.4 %reduce-scatter.11.cloned.1.call-start = ((), (), s32[]{:S(2)}) async-start(), calls=%async_computation.13 | async-start | bytes 2359296 | tf_op jit(solution)/shard_map/reduce_scatter | solution.py:223
  341.8 37.0 %copy-start.1 = (s32[64,128]{1,0:T(8,128)S(1)}, s32[64,128]{1,0:T(8,128)}, u32[]{:S(2)}) copy-start(s32[64,128]{1,0:T(8,128)} %param.10) | copy-start | bytes 98308
Sparse Core Ops, SparseCore 0:
  10.4 37.4 all-gather.2
  120.2 24.0 reduce-scatter.4
  158.4 32.2 all-gather.4
  211.1 34.2 reduce-scatter.8
  299.7 23.0 reduce-scatter.6
  341.9 35.0 reduce-scatter.10

commit v3 on v2

--- a/solution.py
+++ b/solution.py
@@ -1,3 +1,5 @@
+import functools
+
 import jax
 import jax.numpy as jnp
 from jax import lax
@@ -5,6 +7,8 @@
 from jax.experimental.pallas import tpu as pltpu
 from jax.sharding import Mesh
 from jax.sharding import PartitionSpec as P
+
+MESH = pl.DeviceIdType.MESH
 
 CAP = 2
 STEPS = 2
@@ -73,6 +77,57 @@
         return carry
 
     lax.fori_loop(0, arrived_ref.shape[0], body, 0)
+
+
+def edge_exchange_kernel(reduce, x_ref, out_ref, held, send_sem, recv_sem):
+    count = held.shape[0]
+    me = lax.axis_index("edge")
+    barrier = pltpu.get_barrier_semaphore()
+    for d in range(1, count):
+        pl.semaphore_signal(
+            barrier, inc=1, device_id={"edge": lax.rem(me + d, count)}, device_id_type=MESH
+        )
+    pl.semaphore_wait(barrier, count - 1)
+    copies = []
+    for d in range(1, count):
+        peer = lax.rem(me + d, count)
+        copy = pltpu.make_async_remote_copy(
+            src_ref=x_ref.at[peer] if reduce else x_ref.at[0],
+            dst_ref=held.at[me],
+            send_sem=send_sem.at[d],
+            recv_sem=recv_sem.at[d],
+            device_id={"edge": peer},
+            device_id_type=MESH,
+        )
+        copy.start()
+        copies.append(copy)
+    held[me] = x_ref[me] if reduce else x_ref[0]
+    for copy in copies:
+        copy.wait()
+    if reduce:
+        total = held[0]
+        for q in range(1, count):
+            total = total + held[q]
+        out_ref[...] = total
+    else:
+        out_ref[...] = held[...]
+
+
+def edge_exchange(chunks, count, reduce, collective_id):
+    piece = chunks.shape[1:]
+    out_shape = piece if reduce else (count,) + piece
+    return pl.pallas_call(
+        functools.partial(edge_exchange_kernel, reduce),
+        out_shape=jax.ShapeDtypeStruct(out_shape, chunks.dtype),
+        in_specs=[pl.BlockSpec(memory_space=pltpu.VMEM)],
+        out_specs=pl.BlockSpec(memory_space=pltpu.VMEM),
+        scratch_shapes=[
+            pltpu.VMEM((count,) + piece, chunks.dtype),
+            pltpu.SemaphoreType.DMA((count,)),
+            pltpu.SemaphoreType.DMA((count,)),
+        ],
+        compiler_params=pltpu.CompilerParams(collective_id=collective_id, has_side_effects=True),
+    )(chunks)
 
 
 def forward_apply(rows, slots, weights_t, received, quarters, blocks_dev):
@@ -185,7 +240,7 @@
 
     member, group_row = grouping(row_ids, blocks_dev)
     member_slot = jnp.concatenate([placed_slots, jnp.zeros((1,), jnp.int32)])[member]
-    padded = jnp.concatenate([weights, jnp.zeros((1,) + weights.shape[1:], weights.dtype)])[member]
+    padded = jnp.take(weights, member, axis=0, mode="fill", fill_value=0)
     group_count = member.shape[0] // GROUP
     width = weights.shape[2]
     weights_g = padded.reshape(group_count, GROUP * quarter, width)
@@ -205,16 +260,14 @@
             outgoing, ("x", "c"), split_axis=0, concat_axis=0, tiled=True
         )
         partial = forward_apply(group_row, member_slot, weights_t, received, quarters, blocks_dev)
-        summed = lax.psum_scatter(
-            partial.reshape(quarters * row_count, hidden), "edge", scatter_dimension=0, tiled=True
-        )
-        current = 0.9 * summed + 0.1 * teleport
+        summed = edge_exchange(partial, quarters, True, 1)
+        current = 0.9 * summed.reshape(row_count, hidden) + 0.1 * teleport
 
     adjoint = cotangent
     gradient = 0.1 * cotangent
     for step_index in range(STEPS):
         rounded = adjoint.astype(jnp.bfloat16).reshape(1, blocks_dev, quarter, hidden)
-        whole_rows = lax.all_gather(rounded, "edge", axis=0, tiled=True)
+        whole_rows = edge_exchange(rounded, quarters, False, 2)
         slot_sums = backward_apply(group_row, member_slot, weights_g, whole_rows, slot_total)
         arrived = lax.all_to_all(
             slot_sums, ("x", "c"), split_axis=0, concat_axis=0, tiled=True

time: 390 us -> 378 us (0.969)
  waiting for transfers between devices: 172 us -> 101 us
  Pallas kernels: 71.3 us -> 126 us
  other arithmetic: 26.8 us -> 41.5 us
  blocking collectives: 22.7 us -> 36.4 us
  starting transfers between devices: 35.1 us -> 21.7 us
  local copies, waits for them, and re-layouts: 43.3 us -> 36.1 us
    pallas_call x0 -> x4, Pallas kernels: none -> 54.8 us  [edge_exchange(): pl.pallas_call(functools.partial(edge_exchange_kernel, reduce), out_shape...]
    all_to_all x0 -> x1, blocking collectives: none -> 36.4 us  [per_device(): lax.all_to_all(outgoing, ('x', 'c'), split_axis=0, concat_axis=0, tiled=T...]
    all_to_all x2, waiting for transfers between devices: 82.3 us -> 46 us  [per_device(): lax.all_to_all(slot_sums, ('x', 'c'), split_axis=0, concat_axis=0, tiled=...]
    reduce_scatter x2, waiting for transfers between devices: 59.6 us -> 29.9 us  [per_device(): owned = lax.psum_scatter(dense, 'z', scatter_dimension=0, tiled=True)]
    all_gather x2 -> x0, blocking collectives: 22.7 us -> none  [per_device(): whole_rows = lax.all_gather(rounded, 'edge', axis=0, tiled=True)]
    select_n x1 -> x3, other arithmetic: 0.01 us -> 14 us  [per_device(): padded = jnp.take(weights, member, axis=0, mode='fill', fill_value=0)]
    all_to_all x2 -> x1, starting transfers between devices: 14.5 us -> 4.67 us  [per_device(): lax.all_to_all(outgoing, ('x', 'c'), split_axis=0, concat_axis=0, tiled=T...]
    concatenate x1 -> x0, local copies, waits for them, and re-layouts: 6.57 us -> none  [per_device(): jnp.concatenate([weights, jnp.zeros((1,) + weights.shape[1:], weights.dty...]
  transfers between devices with their start and end apart: 10 -> 7, of which waited for: 5 -> 3; matrix products, arithmetic and copies ran while one was open for 16% -> 8% of each run, Pallas kernels for 15% -> 26%
where the time goes in v3:
time: 378 us; the launch traced here: 377 us
  Pallas kernels  126 us (33%)
  waiting for transfers between devices  101 us (27%)
  other arithmetic  41.5 us (11%)
  blocking collectives  36.4 us (10%)
  local copies, waits for them, and re-layouts  36.1 us (10%)
  starting transfers between devices  21.7 us (6%)
  between operations  14 us (4%)
    pallas_call x4, Pallas kernels, edge_exchange(): pl.pallas_call(functools.partial(edge_exchange_kernel, reduce), out_shape...  54.8 us
    all_to_all x2, waiting for transfers between devices, per_device(): lax.all_to_all(slot_sums, ('x', 'c'), split_axis=0, concat_axis=0, tiled=...  46 us
    all_to_all x1, blocking collectives, per_device(): lax.all_to_all(outgoing, ('x', 'c'), split_axis=0, concat_axis=0, tiled=T...  36.4 us
    reduce_scatter x2, waiting for transfers between devices, per_device(): owned = lax.psum_scatter(dense, 'z', scatter_dimension=0, tiled=True)  29.9 us
    pallas_call x2, Pallas kernels, backward_apply(): pl.pallas_call(backward_kernel, out_shape=jax.ShapeDtypeStruct((slot_tota...  29.8 us
    pallas_call x2, Pallas kernels, forward_apply(): pl.pallas_call(forward_kernel, out_shape=jax.ShapeDtypeStruct((quarters,...  27.6 us
    all_gather x2, waiting for transfers between devices, per_device(): line_blocks = lax.all_gather(rounded, 'z', axis=0, tiled=True)  25.2 us
    all_to_all x2, starting transfers between devices, per_device(): lax.all_to_all(slot_sums, ('x', 'c'), split_axis=0, concat_axis=0, tiled=...  17 us
  transfers between devices with their start and end apart: 7, of which 3 were waited for; matrix products, arithmetic and copies ran while one was open for 8% of the time, Pallas kernels for 26%

profile of v3, /device:TPU:1, one launch (start us, length us, event | category | flops | bytes accessed | tf_op | source)
XLA Modules:
  0.0 376.9 jit_solution(7418662322855660538)
XLA Ops:
  7.2 0.8 convert_reduce_fusion
  8.0 3.8 %sort.17 = (s32[192]{0:T(256)}, s32[192]{0:T(256)S(1)}) sort(s32[192]{0:T(256)} %bitcast.58, s32[192]{0:T(256)S(1)} %iota.36), dimensions={0}, to_apply=%region_3.4 | sort | flops 1536 | bytes 3072 | tf_op jit(solution)/shard_map/jit(argsort)/sort | solution.py:193
  11.9 2.0 gather_fusion
  13.9 0.2 reduce-window.17
  14.0 0.2 reduce-window.18
  14.2 0.7 fusion.15
  15.0 8.7 %compare_select_fusion.9 = (s32[192,1]{0,1:T(1,128)S(1)}, s32[192,1]{0,1:T(1,128)S(1)}) fusion(s32[]{:T(128)} %bitcast.17, s32[]{:T(128)} %bitcast.18, s32[]{:T(128)} %bitcast.19, s32[]{:T(128)} %bitcast.20, s32[]{:T(128)} %bitcast.21, s32[]{:T(128)} %bitcast.23, s32[]{:T(128)} %bitcast.22, s32[192,1]{0,1:T(1,128)S(1)} %bitcast.72, s32[]{:T(128)} %bitcast.12, ...), kind=kLoop, calls=%fused_computation.42 | loop fusion | flops 4032 | bytes 2360 | tf_op jit(solution)/shard_map/gather | solution.py:202
  23.7 1.2 broadcast_select_fusion.3
  24.9 1.2 scatter_custom_fusion
  26.1 0.1 convert_reduce_fusion.1
  26.2 0.5 broadcast_minimum_fusion.rows_ref
  26.7 0.7 fusion.5
  27.5 0.1 broadcast_in_dim.64
  27.6 0.1 broadcast_in_dim.70
  27.7 0.1 broadcast_in_dim.71
  27.8 1.6 convert_element_type.23
  29.4 11.8 %shard_map.81.a_ref = bf16[4,8,64,128]{3,2,1,0:T(8,128)(2,1)} custom-call(bf16[1,8,64,128]{3,2,1,0:T(8,128)(2,1)} %bitcast.64), custom_call_target="tpu_custom_call" | custom-call | tf_op jit(solution)/shard_map/pallas_call | solution.py:119
  41.2 0.1 pad_add_fusion
  41.3 2.5 gather_fusion.1
  43.8 11.1 %gather_fusion.2 = bf16[224,64,256]{2,1,0:T(8,128)(2,1)} fusion(bf16[192,64,256]{2,1,0:T(8,128)(2,1)} %bitcast.63, s32[1024]{0:T(1024)S(1)} %pad_clamp_fusion.1), kind=kCustom, calls=%fused_computation.4 | custom fusion | bytes 14680960 | tf_op jit(solution)/shard_map/jit(_take)/gather | solution.py:243
  54.9 7.3 %bitcast_select_fusion.v_ref = bf16[56,256,256]{2,1,0:T(8,128)(2,1)} fusion(pred[56,256]{1,0:T(8,128)(4,1)S(1)} %broadcast_in_dim.71, bf16[56,256,256]{2,1,0:T(8,128)(2,1)} %bitcast.60), kind=kLoop, calls=%fused_computation.7 | loop fusion | flops 3670016 | bytes 14694400 | tf_op jit(solution)/shard_map/jit(_take)/select_n | solution.py:243
  62.3 14.9 %shard_map.82 = f32[128,64,128]{2,1,0:T(8,128)} custom-call(s32[56]{0:T(128)} %broadcast_minimum_fusion.rows_ref, s32[224]{0:T(256)} %gather_fusion.1, bf16[56,256,256]{2,1,0:T(8,128)(2,1)} %bitcast_select_fusion.v_ref, bf16[4,8,64,128]{3,2,1,0:T(8,128)(2,1)} %shard_map.81.a_ref), custom_call_target="tpu_custom_call" | custom-call | tf_op jit(solution)/shard_map/pallas_call | solution.py:157
  77.2 6.7 %all-to-all-start.2 = ((f32[128,64,128]{2,1,0:T(8,128)}), f32[128,64,128]{2,1,0:T(8,128)}, u32[]{:S(2)}, u32[]{:S(2)}) async-start(f32[128,64,128]{2,1,0:T(8,128)} %shard_map.82), calls=%async_computation.2 | async-start | bytes 8388608 | tf_op jit(solution)/shard_map/all_to_all | solution.py:272
  83.8 0.7 convert_element_type.21
  84.5 0.0 all-gather.3.cloned.1.call-update
  84.6 0.0 reduce-scatter.3.cloned.1.call-start
  84.6 0.1 fusion.2
  84.7 0.1 broadcast_or_fusion
  84.8 0.1 reshape.306
  85.0 1.8 gather_fusion.3
  86.7 46.0 %all-to-all-done.2.arrived_ref = f32[128,64,128]{2,1,0:T(8,128)} async-done(((f32[128,64,128]{2,1,0:T(8,128)}), f32[128,64,128]{2,1,0:T(8,128)}, u32[]{:S(2)}, u32[]{:S(2)}) %all-to-all-start.2) | async-done | bytes 4194336 | tf_op jit(solution)/shard_map/all_to_all | solution.py:272
  132.8 6.9 %shard_map.83 = f32[8,8,64,128]{3,2,1,0:T(8,128)} custom-call(s32[128]{0:T(128)} %gather_fusion.3, f32[128,64,128]{2,1,0:T(8,128)} %all-to-all-done.2.arrived_ref), custom_call_target="tpu_custom_call" | custom-call | tf_op jit(solution)/shard_map/pallas_call | solution.py:176
  139.6 0.0 reduce-scatter.3.cloned.1.call-update
  139.7 0.1 add.226
  139.7 0.1 add.227
  139.9 0.0 all-gather.3.cloned.1.call-done
  139.9 2.2 gather_fusion.4
  142.1 1.6 broadcast_select_fusion.1
  143.7 4.7 %all-to-all-start = ((bf16[128,64,128]{2,1,0:T(8,128)(2,1)}), bf16[128,64,128]{2,1,0:T(8,128)(2,1)S(1)}, u32[]{:S(2)}, u32[]{:S(2)}) async-start(bf16[128,64,128]{2,1,0:T(8,128)(2,1)} %broadcast_select_fusion.1), calls=%async_computation | async-start | bytes 4194304 | tf_op jit(solution)/shard_map/all_to_all | solution.py:259
  148.4 29.9 %reduce-scatter.3.cloned.1.call-done = f32[1,8,64,128]{3,2,1,0:T(8,128)} async-done(((f32[8,8,64,128]{3,2,1,0:T(8,128)}), f32[1,8,64,128]{3,2,1,0:T(8,128)}) %reduce-scatter.3.cloned.1.call-update) | async-done | bytes 262160 | tf_op jit(solution)/shard_map/reduce_scatter | solution.py:276
  178.3 1.7 broadcast_multiply_fusion.1
  179.9 9.3 %shard_map.84.a_ref = bf16[4,8,64,128]{3,2,1,0:T(8,128)(2,1)} custom-call(bf16[1,8,64,128]{3,2,1,0:T(8,128)(2,1)} %get-tuple-element.8.x_ref), custom_call_target="tpu_custom_call" | custom-call | tf_op jit(solution)/shard_map/pallas_call | solution.py:119
  189.2 14.9 %shard_map.85 = f32[128,64,128]{2,1,0:T(8,128)} custom-call(s32[56]{0:T(128)} %broadcast_minimum_fusion.rows_ref, s32[224]{0:T(256)} %gather_fusion.1, bf16[56,256,256]{2,1,0:T(8,128)(2,1)} %bitcast_select_fusion.v_ref, bf16[4,8,64,128]{3,2,1,0:T(8,128)(2,1)} %shard_map.84.a_ref), custom_call_target="tpu_custom_call" | custom-call | tf_op jit(solution)/shard_map/pallas_call | solution.py:157
  204.1 1.3 copy-done.2
  205.5 10.3 %all-to-all-start.3 = ((f32[128,64,128]{2,1,0:T(8,128)}), f32[128,64,128]{2,1,0:T(8,128)}, u32[]{:S(2)}, u32[]{:S(2)}) async-start(f32[128,64,128]{2,1,0:T(8,128)} %shard_map.85), calls=%async_computation.4 | async-start | bytes 8388608 | tf_op jit(solution)/shard_map/all_to_all | solution.py:272
  215.8 6.7 %broadcast_select_fusion = bf16[56,4,64,256]{3,2,1,0:T(8,128)(2,1)} fusion(bf16[56,4,64,256]{3,2,1,0:T(8,128)(2,1)} %bitcast.61, pred[56,4]{1,0:T(8,128)(4,1)S(1)} %broadcast_in_dim.64), kind=kLoop, calls=%fused_computation.8 | loop fusion | flops 3670016 | bytes 14680288 | tf_op jit(solution)/shard_map/jit(_take)/select_n | solution.py:243
  222.5 10.4 %copy.14.vt_ref = bf16[56,256,256]{2,1,0:T(8,128)(2,1)} copy(bf16[56,256,256]{1,2,0:T(8,128)(2,1)} %bitcast.62) | data formatting | bytes 14680064 | tf_op jit(solution)/shard_map/reshape | solution.py:250
  232.9 13.8 %shard_map.77.x_ref = f32[4,8,64,128]{3,2,1,0:T(8,128)} custom-call(s32[56]{0:T(128)} %broadcast_minimum_fusion.rows_ref, s32[224]{0:T(256)} %gather_fusion.1, bf16[56,256,256]{2,1,0:T(8,128)(2,1)} %copy.14.vt_ref, bf16[128,64,128]{2,1,0:T(8,128)(2,1)} %copy-done.2), custom_call_target="tpu_custom_call" | custom-call | tf_op jit(solution)/shard_map/pallas_call | solution.py:136
  246.6 17.0 %shard_map.78 = f32[8,64,128]{2,1,0:T(8,128)} custom-call(f32[4,8,64,128]{3,2,1,0:T(8,128)} %shard_map.77.x_ref), custom_call_target="tpu_custom_call" | custom-call | tf_op jit(solution)/shard_map/pallas_call | solution.py:119
  263.7 1.0 broadcast_multiply_fusion.3
  264.6 0.7 fusion
  265.4 0.0 all-gather.5.cloned.1.call-update
  265.4 0.0 reduce-scatter.5.cloned.1.call-start
  265.4 6.9 %shard_map.86 = f32[8,8,64,128]{3,2,1,0:T(8,128)} custom-call(s32[128]{0:T(128)} %gather_fusion.3, f32[128,64,128]{2,1,0:T(8,128)} %all-to-all-done.3.arrived_ref), custom_call_target="tpu_custom_call" | custom-call | tf_op jit(solution)/shard_map/pallas_call | solution.py:176
  272.4 25.2 %all-gather.5.cloned.1.call-done = bf16[64,64,128]{2,1,0:T(8,128)(2,1)} async-done(((bf16[8,64,128]{2,1,0:T(8,128)(2,1)}), bf16[64,64,128]{2,1,0:T(8,128)(2,1)}) %all-gather.5.cloned.1.call-update) | async-done | bytes 1048592 | tf_op jit(solution)/shard_map/all_gather | solution.py:257
  297.5 2.2 gather_fusion.5
  299.7 0.3 broadcast_select_fusion.2
  300.0 36.4 %all_to_all.20.x_ref = bf16[128,64,128]{2,1,0:T(8,128)(2,1)} all-to-all(bf16[128,64,128]{2,1,0:T(8,128)(2,1)S(1)} %broadcast_select_fusion.2), channel_id=1, replica_groups=mesh['z'=8,'x'=4,'c'=2,'edge'=4] {'x','c'}, dimensions={0} | all-to-all | bytes 4194304 | tf_op jit(solution)/shard_map/all_to_all | solution.py:259
  336.4 13.9 %shard_map.79.x_ref = f32[4,8,64,128]{3,2,1,0:T(8,128)} custom-call(s32[56]{0:T(128)} %broadcast_minimum_fusion.rows_ref, s32[224]{0:T(256)} %gather_fusion.1, bf16[56,256,256]{2,1,0:T(8,128)(2,1)} %copy.14.vt_ref, bf16[128,64,128]{2,1,0:T(8,128)(2,1)} %all_to_all.20.x_ref), custom_call_target="tpu_custom_call" | custom-call | tf_op jit(solution)/shard_map/pallas_call | solution.py:136
  350.3 16.6 %shard_map.80 = f32[8,64,128]{2,1,0:T(8,128)} custom-call(f32[4,8,64,128]{3,2,1,0:T(8,128)} %shard_map.79.x_ref), custom_call_target="tpu_custom_call" | custom-call | tf_op jit(solution)/shard_map/pallas_call | solution.py:119
  366.9 1.0 broadcast_multiply_fusion.2
  367.9 0.7 bitcast_add_fusion.2
  368.6 1.0 broadcast_multiply_fusion
  369.6 0.7 bitcast_add_fusion
  (33 shorter events, 0.2 us)
Async XLA Ops:
  7.2 77.8 %copy-start = (s32[64,128]{1,0:T(8,128)S(1)}, s32[64,128]{1,0:T(8,128)}, u32[]{:S(2)}) copy-start(s32[64,128]{1,0:T(8,128)} %param.10) | copy-start | bytes 98308
  77.2 6.7 %copy-start.3 = (f32[512,128]{1,0:T(8,128)S(1)}, f32[512,128]{1,0:T(8,128)}, u32[]{:S(2)}) copy-start(f32[512,128]{1,0:T(8,128)} %param.8) | copy-start | bytes 786436
  77.2 55.6 %all-to-all-start.2 = ((f32[128,64,128]{2,1,0:T(8,128)}), f32[128,64,128]{2,1,0:T(8,128)}, u32[]{:S(2)}, u32[]{:S(2)}) async-start(f32[128,64,128]{2,1,0:T(8,128)} %shard_map.82), calls=%async_computation.2 | async-start | bytes 8388608 | tf_op jit(solution)/shard_map/all_to_all | solution.py:272
  83.8 56.1 %all-gather.3.cloned.1.call-start = ((), (), s32[]{:S(2)}) async-start(), calls=%async_computation.6 | async-start | bytes 1179648 | tf_op jit(solution)/shard_map/all_gather | solution.py:257
  84.6 93.7 %reduce-scatter.3.cloned.1.call-start = ((), (), s32[]{:S(2)}) async-start(), calls=%async_computation.8 | async-start | bytes 2359296 | tf_op jit(solution)/shard_map/reduce_scatter | solution.py:276
  86.7 53.1 %copy-start.4 = (s32[128]{0:T(128)S(1)}, s32[128]{0:T(128)}, u32[]{:S(2)}) copy-start(s32[128]{0:T(128)} %gather_fusion.3) | copy-start | bytes 1540
  143.7 60.4 %all-to-all-start = ((bf16[128,64,128]{2,1,0:T(8,128)(2,1)}), bf16[128,64,128]{2,1,0:T(8,128)(2,1)S(1)}, u32[]{:S(2)}, u32[]{:S(2)}) async-start(bf16[128,64,128]{2,1,0:T(8,128)(2,1)} %broadcast_select_fusion.1), calls=%async_computation | async-start | bytes 4194304 | tf_op jit(solution)/shard_map/all_to_all | solution.py:259
  204.1 1.3 copy-start.2
  205.5 60.0 %all-to-all-start.3 = ((f32[128,64,128]{2,1,0:T(8,128)}), f32[128,64,128]{2,1,0:T(8,128)}, u32[]{:S(2)}, u32[]{:S(2)}) async-start(f32[128,64,128]{2,1,0:T(8,128)} %shard_map.85), calls=%async_computation.4 | async-start | bytes 8388608 | tf_op jit(solution)/shard_map/all_to_all | solution.py:272
  215.8 81.8 %all-gather.5.cloned.1.call-start = ((), (), s32[]{:S(2)}) async-start(), calls=%async_computation.7 | async-start | bytes 1179648 | tf_op jit(solution)/shard_map/all_gather | solution.py:257
  265.4 103.3 %reduce-scatter.5.cloned.1.call-start = ((), (), s32[]{:S(2)}) async-start(), calls=%async_computation.9 | async-start | bytes 2359296 | tf_op jit(solution)/shard_map/reduce_scatter | solution.py:276
  336.4 33.2 %copy-start.5 = (f32[512,128]{1,0:T(8,128)S(1)}, f32[512,128]{1,0:T(8,128)}, u32[]{:S(2)}) copy-start(f32[512,128]{1,0:T(8,128)} %param.9) | copy-start | bytes 786436
  336.4 34.0 %copy-start.1 = (s32[64,128]{1,0:T(8,128)S(1)}, s32[64,128]{1,0:T(8,128)}, u32[]{:S(2)}) copy-start(s32[64,128]{1,0:T(8,128)} %param.10) | copy-start | bytes 98308
Sparse Core Ops, SparseCore 0:
  87.0 36.7 all-gather.2
  139.8 38.4 reduce-scatter.2
  265.5 32.0 all-gather.4
  300.0 41.9 reduce-scatter.4
